TPU v7x, 256 devices: a whole 4x4x8 slice. The times are simulated.
256 devices in a mesh: ctx: 32 (over z, x), tp: 8 (over y, core).
Axes of the slice: x: 4, y: 4, z: 8, core: 2. Of those that a mesh axis runs over, the one named last changes fastest.
Arguments:
- projected: bfloat16 [3, 8192, 4096], P(None, 'ctx', 'tp'), may hold values from -6 to 6
- conv_weight: float32 [3, 4, 4096], P(None, None, 'tp'), may hold values from -3 to 3
- log_decay: float32 [32, 8192], P('tp', 'ctx'), may hold values from -2 to 0
- write_rate: float32 [32, 8192], P('tp', 'ctx'), may hold values from 0 to 1
- doc_bounds: int32 [8, 2], replicated, may hold values from 0 to 64, as said below
- out_gate: bfloat16 [8192, 4096], P('ctx', 'tp'), may hold values from -6 to 6
- norm_gain: float32 [128], replicated, may hold values from 0.1 to 1.9
- out_weight: bfloat16 [4096, 4096], P('tp'), may hold values from -0.09375 to 0.09375
Outputs:
- layer_out: bfloat16 [8192, 4096], P(('ctx', 'tp'))
Inputs may be any that keep to these rules, and one draw needn't show every extreme that they name: `doc_bounds`: row i holds the first block and one past the last block of document i, in units of 128 tokens; rows are in order, row 0 starts at 0, each row starts where the previous one ends, the last ends at 64, and every document has at least one block.
All inputs are finite; a program needn't handle non-finite values.
Results may differ from a plain program's by a relative error of at most 0.017.
Values may be sent and summed in bfloat16 or wider, within the bound.
A program may use at most 64 MiB of HBM per device.

v0:
```python
import jax
import jax.numpy as jnp
from jax import lax
from jax.sharding import PartitionSpec as P

SPAN = 128
KERNEL = 4


def shifted(block, axis, distance):
    devices = range(lax.axis_size(axis))
    route = [(i - distance, i) for i in devices if i - distance in devices]
    return lax.ppermute(block, axis, route)


def product(formula, left_side, right_side):
    return jnp.einsum(formula, left_side, right_side, precision=lax.Precision.HIGHEST)


def narrow_product(formula, left_side, right_side):
    return jnp.einsum(formula, left_side, right_side, preferred_element_type=jnp.float32)


def body(
    projected, conv_weight, log_decay, write_rate, doc_bounds, out_gate, norm_gain, out_weight
):
    tok_rows = projected.shape[1]
    head_cols = projected.shape[2]
    head_count = log_decay.shape[0]
    head_dim = head_cols // head_count
    span_count = tok_rows // SPAN
    ctx_index = lax.axis_index("ctx")
    last_rows = projected[:, tok_rows - (KERNEL - 1) :, :]
    before = shifted(last_rows, "ctx", 1)
    extended = jnp.concatenate([before, projected], axis=1)
    span_ids = ctx_index * span_count + jnp.arange(span_count, dtype=jnp.int32)
    resets = jnp.any(span_ids[:, None] == doc_bounds[None, :, 0], axis=1)
    keep_flag = 1.0 - resets.astype(jnp.float32)
    reset_rows = jnp.repeat(resets, SPAN)
    row_offset = jnp.arange(tok_rows, dtype=jnp.int32) % SPAN
    convolved = jnp.zeros((3, tok_rows, head_cols), jnp.float32)
    for tap_lag in range(KERNEL):
        window = extended[:, KERNEL - 1 - tap_lag : KERNEL - 1 - tap_lag + tok_rows, :].astype(
            jnp.float32
        )
        allowed = jnp.logical_not(reset_rows & (row_offset < tap_lag)).astype(jnp.float32)
        convolved = convolved + conv_weight[:, tap_lag, None, :] * window * allowed[None, :, None]
    activated = jax.nn.silu(convolved).reshape(3, tok_rows, head_count, head_dim)
    query_key = activated[:2]
    query_key = query_key / jnp.sqrt(jnp.sum(query_key * query_key, axis=-1, keepdims=True) + 1e-06)

    def blocks(values):
        return (
            values.astype(jnp.bfloat16)
            .reshape(span_count, SPAN, head_count, head_dim)
            .transpose(2, 0, 1, 3)
        )

    query_half = blocks(query_key[0])
    key_half = blocks(query_key[1])
    value_half = blocks(activated[2])
    queries = query_half.astype(jnp.float32)
    keys_span = key_half.astype(jnp.float32)
    value_vecs = value_half.astype(jnp.float32)
    log_gain = jnp.cumsum(log_decay.reshape(head_count, span_count, SPAN), axis=-1)
    write_rows = write_rate.reshape(head_count, span_count, SPAN)
    later_pos = jnp.arange(SPAN)[:, None]
    earlier_pos = jnp.arange(SPAN)[None, :]
    log_ratio = log_gain[..., :, None] - log_gain[..., None, :]
    strict = later_pos > earlier_pos
    inclusive = later_pos >= earlier_pos
    ratio_strict = jnp.where(strict, jnp.exp(jnp.where(strict, log_ratio, 0.0)), 0.0)
    ratio_incl = jnp.where(inclusive, jnp.exp(jnp.where(inclusive, log_ratio, 0.0)), 0.0)
    decay_in = jnp.exp(log_gain)
    decay_tail = jnp.exp(log_gain[..., -1:] - log_gain)
    strict_part = (
        write_rows[..., :, None]
        * ratio_strict
        * narrow_product("hcik,hcjk->hcij", key_half, key_half)
    )
    identity_span = jnp.eye(SPAN, dtype=jnp.float32)
    powered = strict_part
    inverse = identity_span - strict_part
    for level_idx in range(SPAN.bit_length() - 2):
        powered = product("hcij,hcjk->hcik", powered, powered)
        inverse = product("hcij,hcjk->hcik", inverse, identity_span + powered)
    weighted = product("hcts,hcsk->hctk", inverse, (write_rows * decay_in)[..., None] * keys_span)
    updates = product("hcts,hcsv->hctv", inverse, write_rows[..., None] * value_vecs)
    scores = ratio_incl * narrow_product("hcik,hcjk->hcij", query_half, key_half)
    query_eff = decay_in[..., None] * queries - product("hcts,hcsk->hctk", scores, weighted)
    local_out = product("hcts,hcsv->hctv", scores, updates)
    tail_keys = decay_tail[..., None] * keys_span
    identity_head = jnp.eye(head_dim, dtype=jnp.float32)
    transit = jnp.exp(log_gain[..., -1])[..., None, None] * identity_head - product(
        "hctk,hctj->hckj", weighted, tail_keys
    )
    offset = product("hctv,hctk->hcvk", updates, tail_keys)

    def advance(running, span_item):
        run_transit, run_offset = running
        span_transit, span_offset, keep_now = span_item
        next_transit = keep_now * product("hvk,hkj->hvj", run_transit, span_transit)
        next_offset = keep_now * product("hvk,hkj->hvj", run_offset, span_transit) + span_offset
        return ((next_transit, next_offset), (run_transit, run_offset))

    zeros_state = jnp.zeros((head_count, head_dim, head_dim), jnp.float32)
    initial = (jnp.broadcast_to(identity_head, (head_count, head_dim, head_dim)), zeros_state)
    device_maps, prefix_maps = lax.scan(
        advance, initial, (transit.transpose(1, 0, 2, 3), offset.transpose(1, 0, 2, 3), keep_flag)
    )
    dev_transit, dev_offset = device_maps
    pre_transit, pre_offset = prefix_maps

    def relay(turn_index, running):
        incoming = shifted(running[0].astype(jnp.bfloat16), "ctx", 1).astype(jnp.float32)
        return (product("hvk,hkj->hvj", incoming, dev_transit) + dev_offset, incoming)

    entry_state = lax.fori_loop(0, lax.axis_size("ctx"), relay, (zeros_state, zeros_state))[1]
    states = product("hvk,chkj->chvj", entry_state, pre_transit) + pre_offset
    states = keep_flag[:, None, None, None] * states
    attended = product("hctk,chvk->hctv", query_eff, states) + local_out
    attended = attended.transpose(1, 2, 0, 3).reshape(tok_rows, head_count, head_dim)
    gated = jax.nn.silu(out_gate.astype(jnp.float32).reshape(tok_rows, head_count, head_dim))
    normed = (
        attended
        / jnp.sqrt(jnp.mean(attended * attended, axis=-1, keepdims=True) + 1e-05)
        * norm_gain
        * gated
    )
    normed = normed.astype(jnp.bfloat16).reshape(tok_rows, head_cols)
    return lax.psum_scatter(
        jnp.dot(normed, out_weight, preferred_element_type=jnp.float32).astype(jnp.bfloat16),
        "tp",
        scatter_dimension=0,
        tiled=True,
    )


def solution(mesh):
    in_specs = (
        P(None, "ctx", "tp"),
        P(None, None, "tp"),
        P("tp", "ctx"),
        P("tp", "ctx"),
        P(),
        P("ctx", "tp"),
        P(),
        P("tp", None),
    )
    out_specs = P(("ctx", "tp"), None)
    return jax.shard_map(body, mesh=mesh, in_specs=in_specs, out_specs=out_specs, check_vma=False)
```

profile of v0, /device:TPU:226, one launch (start us, length us, event | category | flops | bytes accessed | tf_op | source)
XLA Modules:
  0.0 463.4 jit_solution(6401192402224270420)
XLA Ops:
  37.7 8.0 %while.30 = (s32[]{:T(128)}, f32[4,128,128]{1,2,0:T(8,128)S(1)}, f32[4,128,128]{1,2,0:T(8,128)S(1)}, f32[2,4,128,128]{2,3,1,0:T(8,128)}, f32[2,4,128,128]{2,3,1,...) while((s32[]{:T(128)}, f32[4,128,128]{1,2,0:T(8,128)S(1)}, ...), condition=%wide.region_4.5_spmd.clone, body=%wide.region_3.4_spmd.clone.sunk | while | flops 201654272 | bytes 4981392 | solution.py:108
  47.2 322.6 %while.31 = (s32[]{:T(128)}, bf16[4,128,128]{2,1,0:T(8,128)(2,1)S(1)}, f32[4,128,128]{2,1,0:T(8,128)}, f32[4,128,128]{2,1,0:T(8,128)S(1)}, f32[4,128,128]{2,1,0:T(8,128)S(1)}, /*index=5*/s32[]{:T(128)}, s32[]{:T(128)}) while((s32[]{:T(128)}, bf16[4,128,128]{2,1,0:T(8,128)(2,1)S(1)}, f32[4,128,128]{2,1,0:T(8,128)}, ...), condition=%wide.region_6.7_spmd.clone, body=%wide.region_5.6_spmd.clone.sunk | while | flops 100925440 | bytes 1966207 | solution.py:118
  75.8 7.0 %collective-permute-done = bf16[4,128,128]{2,1,0:T(8,128)(2,1)S(1)} collective-permute-done((bf16[4,128,128]{2,1,0:T(8,128)(2,1)S(1)}, bf16[4,128,128]{2,1,0:T(8,128)(2,1)S(1)}, u32[]{:S(2)}, u32[]{:S(2)}) %collective-permute-start) | collective-permute-done | bytes 131104 | tf_op jit(solution)/shard_map/while/body/eval_jaxpr/ppermute | solution.py:13
  85.8 7.0 %collective-permute-done = bf16[4,128,128]{2,1,0:T(8,128)(2,1)S(1)} collective-permute-done((bf16[4,128,128]{2,1,0:T(8,128)(2,1)S(1)}, bf16[4,128,128]{2,1,0:T(8,128)(2,1)S(1)}, u32[]{:S(2)}, u32[]{:S(2)}) %collective-permute-start) | collective-permute-done | bytes 131104 | tf_op jit(solution)/shard_map/while/body/eval_jaxpr/ppermute | solution.py:13
  95.9 7.0 %collective-permute-done = bf16[4,128,128]{2,1,0:T(8,128)(2,1)S(1)} collective-permute-done((bf16[4,128,128]{2,1,0:T(8,128)(2,1)S(1)}, bf16[4,128,128]{2,1,0:T(8,128)(2,1)S(1)}, u32[]{:S(2)}, u32[]{:S(2)}) %collective-permute-start) | collective-permute-done | bytes 131104 | tf_op jit(solution)/shard_map/while/body/eval_jaxpr/ppermute | solution.py:13
  105.9 7.6 %collective-permute-done = bf16[4,128,128]{2,1,0:T(8,128)(2,1)S(1)} collective-permute-done((bf16[4,128,128]{2,1,0:T(8,128)(2,1)S(1)}, bf16[4,128,128]{2,1,0:T(8,128)(2,1)S(1)}, u32[]{:S(2)}, u32[]{:S(2)}) %collective-permute-start) | collective-permute-done | bytes 131104 | tf_op jit(solution)/shard_map/while/body/eval_jaxpr/ppermute | solution.py:13
  116.5 8.4 %collective-permute-done = bf16[4,128,128]{2,1,0:T(8,128)(2,1)S(1)} collective-permute-done((bf16[4,128,128]{2,1,0:T(8,128)(2,1)S(1)}, bf16[4,128,128]{2,1,0:T(8,128)(2,1)S(1)}, u32[]{:S(2)}, u32[]{:S(2)}) %collective-permute-start) | collective-permute-done | bytes 131104 | tf_op jit(solution)/shard_map/while/body/eval_jaxpr/ppermute | solution.py:13
  147.7 7.0 %collective-permute-done = bf16[4,128,128]{2,1,0:T(8,128)(2,1)S(1)} collective-permute-done((bf16[4,128,128]{2,1,0:T(8,128)(2,1)S(1)}, bf16[4,128,128]{2,1,0:T(8,128)(2,1)S(1)}, u32[]{:S(2)}, u32[]{:S(2)}) %collective-permute-start) | collective-permute-done | bytes 131104 | tf_op jit(solution)/shard_map/while/body/eval_jaxpr/ppermute | solution.py:13
  157.7 7.0 %collective-permute-done = bf16[4,128,128]{2,1,0:T(8,128)(2,1)S(1)} collective-permute-done((bf16[4,128,128]{2,1,0:T(8,128)(2,1)S(1)}, bf16[4,128,128]{2,1,0:T(8,128)(2,1)S(1)}, u32[]{:S(2)}, u32[]{:S(2)}) %collective-permute-start) | collective-permute-done | bytes 131104 | tf_op jit(solution)/shard_map/while/body/eval_jaxpr/ppermute | solution.py:13
  167.8 7.0 %collective-permute-done = bf16[4,128,128]{2,1,0:T(8,128)(2,1)S(1)} collective-permute-done((bf16[4,128,128]{2,1,0:T(8,128)(2,1)S(1)}, bf16[4,128,128]{2,1,0:T(8,128)(2,1)S(1)}, u32[]{:S(2)}, u32[]{:S(2)}) %collective-permute-start) | collective-permute-done | bytes 131104 | tf_op jit(solution)/shard_map/while/body/eval_jaxpr/ppermute | solution.py:13
  177.8 7.0 %collective-permute-done = bf16[4,128,128]{2,1,0:T(8,128)(2,1)S(1)} collective-permute-done((bf16[4,128,128]{2,1,0:T(8,128)(2,1)S(1)}, bf16[4,128,128]{2,1,0:T(8,128)(2,1)S(1)}, u32[]{:S(2)}, u32[]{:S(2)}) %collective-permute-start) | collective-permute-done | bytes 131104 | tf_op jit(solution)/shard_map/while/body/eval_jaxpr/ppermute | solution.py:13
  187.8 7.7 %collective-permute-done = bf16[4,128,128]{2,1,0:T(8,128)(2,1)S(1)} collective-permute-done((bf16[4,128,128]{2,1,0:T(8,128)(2,1)S(1)}, bf16[4,128,128]{2,1,0:T(8,128)(2,1)S(1)}, u32[]{:S(2)}, u32[]{:S(2)}) %collective-permute-start) | collective-permute-done | bytes 131104 | tf_op jit(solution)/shard_map/while/body/eval_jaxpr/ppermute | solution.py:13
  198.5 8.4 %collective-permute-done = bf16[4,128,128]{2,1,0:T(8,128)(2,1)S(1)} collective-permute-done((bf16[4,128,128]{2,1,0:T(8,128)(2,1)S(1)}, bf16[4,128,128]{2,1,0:T(8,128)(2,1)S(1)}, u32[]{:S(2)}, u32[]{:S(2)}) %collective-permute-start) | collective-permute-done | bytes 131104 | tf_op jit(solution)/shard_map/while/body/eval_jaxpr/ppermute | solution.py:13
  229.6 7.0 %collective-permute-done = bf16[4,128,128]{2,1,0:T(8,128)(2,1)S(1)} collective-permute-done((bf16[4,128,128]{2,1,0:T(8,128)(2,1)S(1)}, bf16[4,128,128]{2,1,0:T(8,128)(2,1)S(1)}, u32[]{:S(2)}, u32[]{:S(2)}) %collective-permute-start) | collective-permute-done | bytes 131104 | tf_op jit(solution)/shard_map/while/body/eval_jaxpr/ppermute | solution.py:13
  239.7 7.0 %collective-permute-done = bf16[4,128,128]{2,1,0:T(8,128)(2,1)S(1)} collective-permute-done((bf16[4,128,128]{2,1,0:T(8,128)(2,1)S(1)}, bf16[4,128,128]{2,1,0:T(8,128)(2,1)S(1)}, u32[]{:S(2)}, u32[]{:S(2)}) %collective-permute-start) | collective-permute-done | bytes 131104 | tf_op jit(solution)/shard_map/while/body/eval_jaxpr/ppermute | solution.py:13
  249.7 7.0 %collective-permute-done = bf16[4,128,128]{2,1,0:T(8,128)(2,1)S(1)} collective-permute-done((bf16[4,128,128]{2,1,0:T(8,128)(2,1)S(1)}, bf16[4,128,128]{2,1,0:T(8,128)(2,1)S(1)}, u32[]{:S(2)}, u32[]{:S(2)}) %collective-permute-start) | collective-permute-done | bytes 131104 | tf_op jit(solution)/shard_map/while/body/eval_jaxpr/ppermute | solution.py:13
  269.8 7.7 %collective-permute-done = bf16[4,128,128]{2,1,0:T(8,128)(2,1)S(1)} collective-permute-done((bf16[4,128,128]{2,1,0:T(8,128)(2,1)S(1)}, bf16[4,128,128]{2,1,0:T(8,128)(2,1)S(1)}, u32[]{:S(2)}, u32[]{:S(2)}) %collective-permute-start) | collective-permute-done | bytes 131104 | tf_op jit(solution)/shard_map/while/body/eval_jaxpr/ppermute | solution.py:13
  280.4 8.4 %collective-permute-done = bf16[4,128,128]{2,1,0:T(8,128)(2,1)S(1)} collective-permute-done((bf16[4,128,128]{2,1,0:T(8,128)(2,1)S(1)}, bf16[4,128,128]{2,1,0:T(8,128)(2,1)S(1)}, u32[]{:S(2)}, u32[]{:S(2)}) %collective-permute-start) | collective-permute-done | bytes 131104 | tf_op jit(solution)/shard_map/while/body/eval_jaxpr/ppermute | solution.py:13
  311.6 7.0 %collective-permute-done = bf16[4,128,128]{2,1,0:T(8,128)(2,1)S(1)} collective-permute-done((bf16[4,128,128]{2,1,0:T(8,128)(2,1)S(1)}, bf16[4,128,128]{2,1,0:T(8,128)(2,1)S(1)}, u32[]{:S(2)}, u32[]{:S(2)}) %collective-permute-start) | collective-permute-done | bytes 131104 | tf_op jit(solution)/shard_map/while/body/eval_jaxpr/ppermute | solution.py:13
  321.6 7.0 %collective-permute-done = bf16[4,128,128]{2,1,0:T(8,128)(2,1)S(1)} collective-permute-done((bf16[4,128,128]{2,1,0:T(8,128)(2,1)S(1)}, bf16[4,128,128]{2,1,0:T(8,128)(2,1)S(1)}, u32[]{:S(2)}, u32[]{:S(2)}) %collective-permute-start) | collective-permute-done | bytes 131104 | tf_op jit(solution)/shard_map/while/body/eval_jaxpr/ppermute | solution.py:13
  331.6 7.0 %collective-permute-done = bf16[4,128,128]{2,1,0:T(8,128)(2,1)S(1)} collective-permute-done((bf16[4,128,128]{2,1,0:T(8,128)(2,1)S(1)}, bf16[4,128,128]{2,1,0:T(8,128)(2,1)S(1)}, u32[]{:S(2)}, u32[]{:S(2)}) %collective-permute-start) | collective-permute-done | bytes 131104 | tf_op jit(solution)/shard_map/while/body/eval_jaxpr/ppermute | solution.py:13
  351.7 7.0 %collective-permute-done = bf16[4,128,128]{2,1,0:T(8,128)(2,1)S(1)} collective-permute-done((bf16[4,128,128]{2,1,0:T(8,128)(2,1)S(1)}, bf16[4,128,128]{2,1,0:T(8,128)(2,1)S(1)}, u32[]{:S(2)}, u32[]{:S(2)}) %collective-permute-start) | collective-permute-done | bytes 131104 | tf_op jit(solution)/shard_map/while/body/eval_jaxpr/ppermute | solution.py:13
  361.7 7.0 %collective-permute-done = bf16[4,128,128]{2,1,0:T(8,128)(2,1)S(1)} collective-permute-done((bf16[4,128,128]{2,1,0:T(8,128)(2,1)S(1)}, bf16[4,128,128]{2,1,0:T(8,128)(2,1)S(1)}, u32[]{:S(2)}, u32[]{:S(2)}) %collective-permute-start) | collective-permute-done | bytes 131104 | tf_op jit(solution)/shard_map/while/body/eval_jaxpr/ppermute | solution.py:13
  379.4 77.1 %reduce-scatter.2.cloned.1.call-done = bf16[32,4096]{1,0:T(8,128)(2,1)} async-done(((bf16[256,4096]{1,0:T(8,128)(2,1)}), bf16[32,4096]{1,0:T(8,128)(2,1)}) %reduce-scatter.2.cloned.1.call-update) | async-done | bytes 262160 | tf_op jit(solution)/shard_map/reduce_scatter | solution.py:131
  (244 shorter events, 217.2 us)
Async XLA Ops:
  6.5 450.0 %reduce-scatter.2.cloned.1.call-start = ((), (), s32[]{:S(2)}) async-start(), calls=%async_computation.1 | async-start | bytes 2359296 | tf_op jit(solution)/shard_map/reduce_scatter | solution.py:131
  63.8 9.0 %collective-permute-start = (bf16[4,128,128]{2,1,0:T(8,128)(2,1)S(1)}, bf16[4,128,128]{2,1,0:T(8,128)(2,1)S(1)}, u32[]{:S(2)}, u32[]{:S(2)}) collective-permute-start(bf16[4,128,128]{2,1,0:T(8,128)(2,1)S(1)} %select_convert_fusion.2), channel_id=1, source_target_pairs={{0,8},{8,16},{16,24},{24,32},{32,40},{40,48},{48,56},{56,64},{64,7... | collective-permute-start | bytes 393224 | tf_op jit(solution)/shard_map/while/body/eval_jaxpr/ppermute | solution.py:13
  73.9 9.0 %collective-permute-start = (bf16[4,128,128]{2,1,0:T(8,128)(2,1)S(1)}, bf16[4,128,128]{2,1,0:T(8,128)(2,1)S(1)}, u32[]{:S(2)}, u32[]{:S(2)}) collective-permute-start(bf16[4,128,128]{2,1,0:T(8,128)(2,1)S(1)} %select_convert_fusion.2), channel_id=1, source_target_pairs={{0,8},{8,16},{16,24},{24,32},{32,40},{40,48},{48,56},{56,64},{64,7... | collective-permute-start | bytes 393224 | tf_op jit(solution)/shard_map/while/body/eval_jaxpr/ppermute | solution.py:13
  83.9 9.0 %collective-permute-start = (bf16[4,128,128]{2,1,0:T(8,128)(2,1)S(1)}, bf16[4,128,128]{2,1,0:T(8,128)(2,1)S(1)}, u32[]{:S(2)}, u32[]{:S(2)}) collective-permute-start(bf16[4,128,128]{2,1,0:T(8,128)(2,1)S(1)} %select_convert_fusion.2), channel_id=1, source_target_pairs={{0,8},{8,16},{16,24},{24,32},{32,40},{40,48},{48,56},{56,64},{64,7... | collective-permute-start | bytes 393224 | tf_op jit(solution)/shard_map/while/body/eval_jaxpr/ppermute | solution.py:13
  93.9 9.0 %collective-permute-start = (bf16[4,128,128]{2,1,0:T(8,128)(2,1)S(1)}, bf16[4,128,128]{2,1,0:T(8,128)(2,1)S(1)}, u32[]{:S(2)}, u32[]{:S(2)}) collective-permute-start(bf16[4,128,128]{2,1,0:T(8,128)(2,1)S(1)} %select_convert_fusion.2), channel_id=1, source_target_pairs={{0,8},{8,16},{16,24},{24,32},{32,40},{40,48},{48,56},{56,64},{64,7... | collective-permute-start | bytes 393224 | tf_op jit(solution)/shard_map/while/body/eval_jaxpr/ppermute | solution.py:13
  104.0 9.5 %collective-permute-start = (bf16[4,128,128]{2,1,0:T(8,128)(2,1)S(1)}, bf16[4,128,128]{2,1,0:T(8,128)(2,1)S(1)}, u32[]{:S(2)}, u32[]{:S(2)}) collective-permute-start(bf16[4,128,128]{2,1,0:T(8,128)(2,1)S(1)} %select_convert_fusion.2), channel_id=1, source_target_pairs={{0,8},{8,16},{16,24},{24,32},{32,40},{40,48},{48,56},{56,64},{64,7... | collective-permute-start | bytes 393224 | tf_op jit(solution)/shard_map/while/body/eval_jaxpr/ppermute | solution.py:13
  114.6 10.3 %collective-permute-start = (bf16[4,128,128]{2,1,0:T(8,128)(2,1)S(1)}, bf16[4,128,128]{2,1,0:T(8,128)(2,1)S(1)}, u32[]{:S(2)}, u32[]{:S(2)}) collective-permute-start(bf16[4,128,128]{2,1,0:T(8,128)(2,1)S(1)} %select_convert_fusion.2), channel_id=1, source_target_pairs={{0,8},{8,16},{16,24},{24,32},{32,40},{40,48},{48,56},{56,64},{64,7... | collective-permute-start | bytes 393224 | tf_op jit(solution)/shard_map/while/body/eval_jaxpr/ppermute | solution.py:13
  145.8 9.0 %collective-permute-start = (bf16[4,128,128]{2,1,0:T(8,128)(2,1)S(1)}, bf16[4,128,128]{2,1,0:T(8,128)(2,1)S(1)}, u32[]{:S(2)}, u32[]{:S(2)}) collective-permute-start(bf16[4,128,128]{2,1,0:T(8,128)(2,1)S(1)} %select_convert_fusion.2), channel_id=1, source_target_pairs={{0,8},{8,16},{16,24},{24,32},{32,40},{40,48},{48,56},{56,64},{64,7... | collective-permute-start | bytes 393224 | tf_op jit(solution)/shard_map/while/body/eval_jaxpr/ppermute | solution.py:13
  155.8 9.0 %collective-permute-start = (bf16[4,128,128]{2,1,0:T(8,128)(2,1)S(1)}, bf16[4,128,128]{2,1,0:T(8,128)(2,1)S(1)}, u32[]{:S(2)}, u32[]{:S(2)}) collective-permute-start(bf16[4,128,128]{2,1,0:T(8,128)(2,1)S(1)} %select_convert_fusion.2), channel_id=1, source_target_pairs={{0,8},{8,16},{16,24},{24,32},{32,40},{40,48},{48,56},{56,64},{64,7... | collective-permute-start | bytes 393224 | tf_op jit(solution)/shard_map/while/body/eval_jaxpr/ppermute | solution.py:13
  165.8 9.0 %collective-permute-start = (bf16[4,128,128]{2,1,0:T(8,128)(2,1)S(1)}, bf16[4,128,128]{2,1,0:T(8,128)(2,1)S(1)}, u32[]{:S(2)}, u32[]{:S(2)}) collective-permute-start(bf16[4,128,128]{2,1,0:T(8,128)(2,1)S(1)} %select_convert_fusion.2), channel_id=1, source_target_pairs={{0,8},{8,16},{16,24},{24,32},{32,40},{40,48},{48,56},{56,64},{64,7... | collective-permute-start | bytes 393224 | tf_op jit(solution)/shard_map/while/body/eval_jaxpr/ppermute | solution.py:13
  175.9 9.0 %collective-permute-start = (bf16[4,128,128]{2,1,0:T(8,128)(2,1)S(1)}, bf16[4,128,128]{2,1,0:T(8,128)(2,1)S(1)}, u32[]{:S(2)}, u32[]{:S(2)}) collective-permute-start(bf16[4,128,128]{2,1,0:T(8,128)(2,1)S(1)} %select_convert_fusion.2), channel_id=1, source_target_pairs={{0,8},{8,16},{16,24},{24,32},{32,40},{40,48},{48,56},{56,64},{64,7... | collective-permute-start | bytes 393224 | tf_op jit(solution)/shard_map/while/body/eval_jaxpr/ppermute | solution.py:13
  185.9 9.6 %collective-permute-start = (bf16[4,128,128]{2,1,0:T(8,128)(2,1)S(1)}, bf16[4,128,128]{2,1,0:T(8,128)(2,1)S(1)}, u32[]{:S(2)}, u32[]{:S(2)}) collective-permute-start(bf16[4,128,128]{2,1,0:T(8,128)(2,1)S(1)} %select_convert_fusion.2), channel_id=1, source_target_pairs={{0,8},{8,16},{16,24},{24,32},{32,40},{40,48},{48,56},{56,64},{64,7... | collective-permute-start | bytes 393224 | tf_op jit(solution)/shard_map/while/body/eval_jaxpr/ppermute | solution.py:13
  196.5 10.3 %collective-permute-start = (bf16[4,128,128]{2,1,0:T(8,128)(2,1)S(1)}, bf16[4,128,128]{2,1,0:T(8,128)(2,1)S(1)}, u32[]{:S(2)}, u32[]{:S(2)}) collective-permute-start(bf16[4,128,128]{2,1,0:T(8,128)(2,1)S(1)} %select_convert_fusion.2), channel_id=1, source_target_pairs={{0,8},{8,16},{16,24},{24,32},{32,40},{40,48},{48,56},{56,64},{64,7... | collective-permute-start | bytes 393224 | tf_op jit(solution)/shard_map/while/body/eval_jaxpr/ppermute | solution.py:13
  227.7 9.0 %collective-permute-start = (bf16[4,128,128]{2,1,0:T(8,128)(2,1)S(1)}, bf16[4,128,128]{2,1,0:T(8,128)(2,1)S(1)}, u32[]{:S(2)}, u32[]{:S(2)}) collective-permute-start(bf16[4,128,128]{2,1,0:T(8,128)(2,1)S(1)} %select_convert_fusion.2), channel_id=1, source_target_pairs={{0,8},{8,16},{16,24},{24,32},{32,40},{40,48},{48,56},{56,64},{64,7... | collective-permute-start | bytes 393224 | tf_op jit(solution)/shard_map/while/body/eval_jaxpr/ppermute | solution.py:13
  237.7 9.0 %collective-permute-start = (bf16[4,128,128]{2,1,0:T(8,128)(2,1)S(1)}, bf16[4,128,128]{2,1,0:T(8,128)(2,1)S(1)}, u32[]{:S(2)}, u32[]{:S(2)}) collective-permute-start(bf16[4,128,128]{2,1,0:T(8,128)(2,1)S(1)} %select_convert_fusion.2), channel_id=1, source_target_pairs={{0,8},{8,16},{16,24},{24,32},{32,40},{40,48},{48,56},{56,64},{64,7... | collective-permute-start | bytes 393224 | tf_op jit(solution)/shard_map/while/body/eval_jaxpr/ppermute | solution.py:13
  247.8 9.0 %collective-permute-start = (bf16[4,128,128]{2,1,0:T(8,128)(2,1)S(1)}, bf16[4,128,128]{2,1,0:T(8,128)(2,1)S(1)}, u32[]{:S(2)}, u32[]{:S(2)}) collective-permute-start(bf16[4,128,128]{2,1,0:T(8,128)(2,1)S(1)} %select_convert_fusion.2), channel_id=1, source_target_pairs={{0,8},{8,16},{16,24},{24,32},{32,40},{40,48},{48,56},{56,64},{64,7... | collective-permute-start | bytes 393224 | tf_op jit(solution)/shard_map/while/body/eval_jaxpr/ppermute | solution.py:13
  257.8 9.0 %collective-permute-start = (bf16[4,128,128]{2,1,0:T(8,128)(2,1)S(1)}, bf16[4,128,128]{2,1,0:T(8,128)(2,1)S(1)}, u32[]{:S(2)}, u32[]{:S(2)}) collective-permute-start(bf16[4,128,128]{2,1,0:T(8,128)(2,1)S(1)} %select_convert_fusion.2), channel_id=1, source_target_pairs={{0,8},{8,16},{16,24},{24,32},{32,40},{40,48},{48,56},{56,64},{64,7... | collective-permute-start | bytes 393224 | tf_op jit(solution)/shard_map/while/body/eval_jaxpr/ppermute | solution.py:13
  267.8 9.6 %collective-permute-start = (bf16[4,128,128]{2,1,0:T(8,128)(2,1)S(1)}, bf16[4,128,128]{2,1,0:T(8,128)(2,1)S(1)}, u32[]{:S(2)}, u32[]{:S(2)}) collective-permute-start(bf16[4,128,128]{2,1,0:T(8,128)(2,1)S(1)} %select_convert_fusion.2), channel_id=1, source_target_pairs={{0,8},{8,16},{16,24},{24,32},{32,40},{40,48},{48,56},{56,64},{64,7... | collective-permute-start | bytes 393224 | tf_op jit(solution)/shard_map/while/body/eval_jaxpr/ppermute | solution.py:13
  278.5 10.3 %collective-permute-start = (bf16[4,128,128]{2,1,0:T(8,128)(2,1)S(1)}, bf16[4,128,128]{2,1,0:T(8,128)(2,1)S(1)}, u32[]{:S(2)}, u32[]{:S(2)}) collective-permute-start(bf16[4,128,128]{2,1,0:T(8,128)(2,1)S(1)} %select_convert_fusion.2), channel_id=1, source_target_pairs={{0,8},{8,16},{16,24},{24,32},{32,40},{40,48},{48,56},{56,64},{64,7... | collective-permute-start | bytes 393224 | tf_op jit(solution)/shard_map/while/body/eval_jaxpr/ppermute | solution.py:13
  309.6 9.0 %collective-permute-start = (bf16[4,128,128]{2,1,0:T(8,128)(2,1)S(1)}, bf16[4,128,128]{2,1,0:T(8,128)(2,1)S(1)}, u32[]{:S(2)}, u32[]{:S(2)}) collective-permute-start(bf16[4,128,128]{2,1,0:T(8,128)(2,1)S(1)} %select_convert_fusion.2), channel_id=1, source_target_pairs={{0,8},{8,16},{16,24},{24,32},{32,40},{40,48},{48,56},{56,64},{64,7... | collective-permute-start | bytes 393224 | tf_op jit(solution)/shard_map/while/body/eval_jaxpr/ppermute | solution.py:13
  319.7 9.0 %collective-permute-start = (bf16[4,128,128]{2,1,0:T(8,128)(2,1)S(1)}, bf16[4,128,128]{2,1,0:T(8,128)(2,1)S(1)}, u32[]{:S(2)}, u32[]{:S(2)}) collective-permute-start(bf16[4,128,128]{2,1,0:T(8,128)(2,1)S(1)} %select_convert_fusion.2), channel_id=1, source_target_pairs={{0,8},{8,16},{16,24},{24,32},{32,40},{40,48},{48,56},{56,64},{64,7... | collective-permute-start | bytes 393224 | tf_op jit(solution)/shard_map/while/body/eval_jaxpr/ppermute | solution.py:13
  329.7 9.0 %collective-permute-start = (bf16[4,128,128]{2,1,0:T(8,128)(2,1)S(1)}, bf16[4,128,128]{2,1,0:T(8,128)(2,1)S(1)}, u32[]{:S(2)}, u32[]{:S(2)}) collective-permute-start(bf16[4,128,128]{2,1,0:T(8,128)(2,1)S(1)} %select_convert_fusion.2), channel_id=1, source_target_pairs={{0,8},{8,16},{16,24},{24,32},{32,40},{40,48},{48,56},{56,64},{64,7... | collective-permute-start | bytes 393224 | tf_op jit(solution)/shard_map/while/body/eval_jaxpr/ppermute | solution.py:13
  349.8 9.0 %collective-permute-start = (bf16[4,128,128]{2,1,0:T(8,128)(2,1)S(1)}, bf16[4,128,128]{2,1,0:T(8,128)(2,1)S(1)}, u32[]{:S(2)}, u32[]{:S(2)}) collective-permute-start(bf16[4,128,128]{2,1,0:T(8,128)(2,1)S(1)} %select_convert_fusion.2), channel_id=1, source_target_pairs={{0,8},{8,16},{16,24},{24,32},{32,40},{40,48},{48,56},{56,64},{64,7... | collective-permute-start | bytes 393224 | tf_op jit(solution)/shard_map/while/body/eval_jaxpr/ppermute | solution.py:13
  359.8 9.0 %collective-permute-start = (bf16[4,128,128]{2,1,0:T(8,128)(2,1)S(1)}, bf16[4,128,128]{2,1,0:T(8,128)(2,1)S(1)}, u32[]{:S(2)}, u32[]{:S(2)}) collective-permute-start(bf16[4,128,128]{2,1,0:T(8,128)(2,1)S(1)} %select_convert_fusion.2), channel_id=1, source_target_pairs={{0,8},{8,16},{16,24},{24,32},{32,40},{40,48},{48,56},{56,64},{64,7... | collective-permute-start | bytes 393224 | tf_op jit(solution)/shard_map/while/body/eval_jaxpr/ppermute | solution.py:13
  (18 other events, 749.4 us)
Sparse Core Ops, SparseCore 0:
  379.5 76.9 reduce-scatter.1
where the time goes:
time: 467 us; the launch traced here: 463 us
  waiting for transfers between devices  301 us (64%)
  starting transfers between devices  67.9 us (15%)
  matrix products  35.7 us (8%)
  other arithmetic  34.6 us (7%)
  between operations  13.9 us (3%)
  local copies, waits for them, and re-layouts  8.79 us (2%)
    ppermute x33, waiting for transfers between devices, shifted(): return lax.ppermute(block, axis, route)  224 us
    reduce_scatter x1, waiting for transfers between devices, body(): lax.psum_scatter(jnp.dot(normed, out_weight, preferred_element_type=jnp.f...  77.1 us
    ppermute x33, starting transfers between devices, shifted(): return lax.ppermute(block, axis, route)  67.9 us
    dot_general x56, matrix products, product(): jnp.einsum(formula, left_side, right_side, precision=lax.Precision.HIGHEST)  30.1 us
    convert_element_type x32, other arithmetic, relay(): shifted(running[0].astype(jnp.bfloat16), 'ctx', 1).astype(jnp.float32)  23.1 us
  transfers between devices with their start and end apart: 34, of which 33 were waited for; matrix products, arithmetic and copies ran while one was open for 1% of the time, Pallas kernels for 0%

commit v1 on v0

v1 whole, which is shorter than its diff:
```python
import functools

import jax
import jax.numpy as jnp
from jax import lax
from jax.experimental import pallas as pl
from jax.experimental.pallas import tpu as pltpu
from jax.sharding import PartitionSpec as P

MESH = pl.DeviceIdType.MESH
F32 = jnp.float32
BF16 = jnp.bfloat16
SPAN = 128
TAPS = 4
NX = 4
NY = 4
HEADS = 4
NP = 8
BLK = 512
NBLK = 8
RCH = 2


def mm(a, b):
    return lax.dot_general(a, b, (((1,), (0,)), ((), ())), preferred_element_type=F32)


def mmt(a, b):
    return lax.dot_general(a, b, (((1,), (1,)), ((), ())), preferred_element_type=F32)


def silu(u):
    return u / (1.0 + jnp.exp(-u))


def kernel(
    nz, proj_hbm, cw_ref, ld_ref, wr_ref, db_ref, gate_hbm, gain_ref, w_hbm, out_ref,
    proj, halo, ext, gate, w_own, w_par,
    gbuf, cbuf, masks, kq, rt, vtmp, lb, pb_s, xb, yb, wub, wts, t1o1, t2, o2, tos, tin,
    pt, po, rowt, rowo, srx, snd, es, ein, qfin, lfin, sg,
    nb, nrx, acc, pb, rxo, rx1, rx2, cs,
    lsem, hsem, wsem, xs_sem, xr_sem, zs_sem, zr_sem, es_sem, er_sem, ns_sem, nr_sem, rs_sem, rr_sem,
):
    ctx = lax.axis_index("ctx")
    tp = lax.axis_index("tp")
    z, x = lax.div(ctx, NX), lax.rem(ctx, NX)
    y, core = lax.div(tp, 2), lax.rem(tp, 2)
    nctx = nz * NX
    nxt = lax.rem(ctx + 1, nctx)
    prv = lax.rem(ctx + nctx - 1, nctx)
    zup = lax.rem(z + 1, nz)
    zdn = lax.rem(z + nz - 1, nz)
    right = lax.rem(y + 1, NY)
    left = lax.rem(y + NY - 1, NY)
    opp = lax.rem(y + 2, NY)
    other = 1 - core

    def remote(src, dst, ssem, rsem, device):
        return pltpu.make_async_remote_copy(
            src_ref=src, dst_ref=dst, send_sem=ssem, recv_sem=rsem,
            device_id=device, device_id_type=MESH,
        )

    barrier = pltpu.get_barrier_semaphore()
    peers = [(nxt, tp), (prv, tp)]
    peers += [(z * NX + lax.rem(x + r, NX), tp) for r in range(1, NX)]
    peers += [(zup * NX + x, tp), (zdn * NX + x, tp)]
    peers += [(ctx, right * 2 + core), (ctx, left * 2 + core), (ctx, y * 2 + other)]
    for device in peers:
        pl.semaphore_signal(barrier, inc=1, device_id=device, device_id_type=MESH)

    loads = [
        pltpu.make_async_copy(proj_hbm, proj, lsem.at[0]),
        pltpu.make_async_copy(gate_hbm, gate, lsem.at[1]),
        pltpu.make_async_copy(w_hbm, w_own, lsem.at[2]),
    ]
    loads[0].start()

    pl.semaphore_wait(barrier, len(peers))
    rows = proj_hbm.shape[1]
    halo_copy = remote(proj_hbm.at[:, pl.ds(rows - 16, 16), :], halo, hsem.at[0], hsem.at[1], (nxt, tp))
    halo_copy.start()
    loads[1].start()
    loads[2].start()
    w_copy = remote(w_hbm, w_par, wsem.at[0], wsem.at[1], (ctx, y * 2 + other))
    w_copy.start()

    gbuf[...] = jnp.zeros((128, 128), F32)
    gbuf[0:4, :] = ld_ref[:, 0:128]
    gbuf[4:8, :] = ld_ref[:, 128:256]
    gbuf[8:12, :] = wr_ref[:, 0:128]
    gbuf[12:16, :] = wr_ref[:, 128:256]
    run = gbuf[0:8, :]
    lane = lax.broadcasted_iota(jnp.int32, (8, 128), 1)
    for step in (1, 2, 4, 8, 16, 32, 64):
        run = run + jnp.where(lane >= step, pltpu.roll(run, step, 1), 0.0)
    gbuf[0:8, :] = run
    cbuf[...] = gbuf[...].T

    row_i = lax.broadcasted_iota(jnp.int32, (128, 128), 0)
    col_i = lax.broadcasted_iota(jnp.int32, (128, 128), 1)
    eye = row_i == col_i
    eye_f = jnp.where(eye, 1.0, 0.0)
    for level in range(1, 7):
        low = lax.shift_right_logical(row_i, level)
        low_j = lax.shift_right_logical(col_i, level)
        same = lax.shift_right_logical(row_i, level + 1) == lax.shift_right_logical(col_i, level + 1)
        masks[level - 1] = jnp.where(same & (low > low_j), 1.0, 0.0).astype(BF16)

    keeps = []
    for span in range(2):
        hit = jnp.int32(0)
        for d in range(db_ref.shape[0]):
            hit = hit + jnp.where(db_ref[d, 0] == ctx * 2 + span, 1, 0)
        keeps.append(1.0 - jnp.minimum(hit, 1).astype(F32))

    ones = jnp.full((128, 128), 1.0, BF16)

    def conv_span(span):
        base = span * SPAN
        for s in (1, 2, 0):
            if span == 0:
                before = halo[s, 8:16, :].astype(F32)
            else:
                before = proj[s, base - 8 : base, :].astype(F32)
            ext[s, 0:8, :] = before * keeps[span]
            ext[s, 8:136, :] = proj[s, base : base + SPAN, :].astype(F32)
            for h in range(HEADS):
                p = span * HEADS + h
                cols = pl.ds(h * 128, 128)
                u = cw_ref[s, 0:1, cols] * ext[s, 8:136, cols]
                for j in range(1, TAPS):
                    u = u + cw_ref[s, j : j + 1, cols] * ext[s, 8 - j : 136 - j, cols]
                a = silu(u)
                if s == 2:
                    rt[p, 128:256, :] = (a.T * gbuf[8 + p : 9 + p, :]).astype(BF16)
                else:
                    ss = mm((a * a).astype(BF16), ones)
                    n = a * lax.rsqrt(ss + 1e-06)
                    nbf = n.astype(BF16)
                    if s == 1:
                        kq[p, 0:128, :] = nbf
                        scale = gbuf[8 + p : 9 + p, :] * jnp.exp(gbuf[p : p + 1, :])
                        rt[p, 0:128, :] = (nbf.astype(F32).T * scale).astype(BF16)
                    else:
                        kq[p, 128:256, :] = nbf

    def scores(p):
        a = mmt(kq[p], kq[p, 0:128, :])
        gcol = jnp.broadcast_to(cbuf[:, p : p + 1], (128, 128))
        bcol = jnp.broadcast_to(cbuf[:, 8 + p : 9 + p], (128, 128))
        dm = jnp.exp(jnp.minimum(gcol - gbuf[p : p + 1, :], 0.0))
        low = jnp.where(row_i > col_i, bcol * dm * a[0:128], 0.0)
        lb[p] = low.astype(BF16)
        pb_s[p] = jnp.where(row_i >= col_i, dm * a[128:256], 0.0).astype(BF16)
        pair = lax.shift_right_logical(row_i, 1) == lax.shift_right_logical(col_i, 1)
        xb[p] = (eye_f - jnp.where(pair, low, 0.0)).astype(BF16)

    loads[0].wait()
    conv_span(1)
    halo_copy.wait()
    conv_span(0)
    for p in range(NP):
        scores(p)
    for level in range(1, 7):
        for p in range(NP):
            yb[p] = mm(xb[p], lb[p] * masks[level - 1]).astype(BF16)
        for p in range(NP):
            xb[p] = xb[p] - mm(yb[p], xb[p]).astype(BF16)
    for p in range(NP):
        wu = mmt(rt[p], xb[p])
        wub[p] = wu.astype(BF16)
        g = gbuf[p : p + 1, :]
        wts[p] = (wu * jnp.exp(g[:, 127:128] - g)).astype(BF16)
    for h in range(HEADS):
        for span in range(2):
            p = span * HEADS + h
            to = mm(wts[p], kq[p, 0:128, :])
            last = jnp.exp(gbuf[p : p + 1, 127:128])
            t = keeps[span] * (last * eye_f - to[0:128])
            if span == 0:
                t1o1[h, 0:128, :] = t.astype(BF16)
                t1o1[h, 128:256, :] = to[128:256].astype(BF16)
            else:
                t2[h] = t.astype(BF16)
                o2[h] = to[128:256]
    for h in range(HEADS):
        d = mm(t1o1[h], t2[h])
        tos[h, 0:128, :] = d[0:128].astype(BF16)
        tos[h, 128:256, :] = (d[128:256] + o2[h]).astype(BF16)

    x_copies = []
    for r in range(1, NX):
        to_x = lax.rem(x + r, NX)
        copy = remote(tos.at[to_x], tin.at[x], xs_sem.at[r - 1], xr_sem.at[r - 1], (z * NX + to_x, tp))
        copy.start()
        x_copies.append(copy)
    tin[x] = tos[x]

    for h in range(HEADS):
        for span in range(2):
            p = span * HEADS + h
            pw = mmt(pb_s[p], wub[p])
            gcol = jnp.broadcast_to(cbuf[:, p : p + 1], (128, 128))
            q = keeps[span] * (jnp.exp(gcol) * kq[p, 128:256, :].astype(F32) - pw[:, 0:128])
            if span == 0:
                qfin[h, 0:128, :] = q.astype(BF16)
                lfin[h, 0:128, :] = pw[:, 128:256]
            else:
                q2 = mmt(q.astype(BF16), t1o1[h])
                qfin[h, 128:256, :] = q2[:, 0:128].astype(BF16)
                lfin[h, 128:256, :] = pw[:, 128:256] + q2[:, 128:256]
    loads[1].wait()
    for h in range(HEADS):
        cols = pl.ds(h * 128, 128)
        sg[h] = silu(gate[:, cols].astype(F32)) * gain_ref[0:1, :]

    for copy in x_copies:
        copy.wait()

    pt[0] = eye_f.astype(BF16)
    po[0] = jnp.zeros((128, 128), F32)
    pt[1] = tin[0, 0:128, :]
    po[1] = tin[0, 128:256, :].astype(F32)
    cur = tin[0]
    for j in range(1, NX):
        step = mm(cur, tin[j, 0:128, :])
        off = step[128:256] + tin[j, 128:256, :].astype(F32)
        if j < NX - 1:
            pt[j + 1] = step[0:128].astype(BF16)
            po[j + 1] = off
            cur = jnp.concatenate([step[0:128], off], axis=0).astype(BF16)
        else:
            rowt[...] = step[0:128].astype(BF16)
            rowo[...] = off

    crows = 128 // RCH

    def z_copy(i):
        part = pl.ds(i * crows, crows)
        return remote(snd.at[part, :], srx.at[part, :], zs_sem.at[i], zr_sem.at[i], (zup * NX + x, tp))

    @pl.when(z == 0)
    def _():
        srx[...] = jnp.zeros((128, 128), BF16)

    for i in range(RCH):
        @pl.when(z > 0)
        def _():
            z_copy(i).wait_recv()

        part = pl.ds(i * crows, crows)
        snd[part, :] = (mm(srx[part, :], rowt[...]) + rowo[part, :]).astype(BF16)

        @pl.when(z < nz - 1)
        def _():
            z_copy(i).start()

    e_copies = []
    for r in range(1, NX):
        to_x = lax.rem(x + r, NX)
        es[r - 1] = (mm(srx[...], pt[to_x]) + po[to_x]).astype(BF16)
        copy = remote(es.at[r - 1], ein.at[x], es_sem.at[r - 1], er_sem.at[r - 1], (z * NX + to_x, tp))
        copy.start()
        e_copies.append(copy)
    ein[x] = (mm(srx[...], pt[x]) + po[x]).astype(BF16)

    mean_ones = jnp.full((128, 128), 1.0 / 128.0, BF16)
    n_copies = []
    for r in range(NX):
        head = lax.rem(x + NX - r, NX)
        if r > 0:
            e_copies[r - 1].wait_recv()
        att = mmt(qfin[head], ein[head]) + lfin[head]
        ms = mm((att * att).astype(BF16), mean_ones)
        nrm = (att * lax.rsqrt(ms + 1e-05) * sg[head]).astype(BF16)
        cols = pl.ds(pl.multiple_of(head * 128, 128), 128)
        for c in range(2):
            for b in range(NY):
                lo = b * 64 + c * 32
                nb[c, b * 32 : b * 32 + 32, cols] = nrm[lo : lo + 32, :]
        copy = remote(
            nb.at[other, :, cols], nrx.at[:, cols], ns_sem.at[r], nr_sem.at[r], (ctx, y * 2 + other)
        )
        copy.start()
        n_copies.append(copy)

    loads[2].wait()
    for b in range(NBLK):
        cols = pl.ds(b * BLK, BLK)
        acc[:, cols] = mm(nb[core], w_own[:, cols])
    w_copy.wait()
    for copy in n_copies:
        copy.wait()

    order = (0, 4, 1, 5, 2, 6, 3, 7)
    half = NBLK // 2
    o_copies, d_copies, c_copies = {}, {}, {}
    for b in order:
        cols = pl.ds(b * BLK, BLK)
        res = (acc[:, cols] + mm(nrx[...], w_par[:, cols])).astype(BF16)
        for d in range(NY):
            pb[b, d] = res[d * 32 : d * 32 + 32, :]
        first, second = (right, left) if b < half else (left, right)
        o_copies[b] = remote(
            pb.at[b, opp], rxo.at[b], rs_sem.at[0, b], rr_sem.at[0, b], (ctx, first * 2 + core)
        )
        o_copies[b].start()
        d_copies[b] = remote(
            pb.at[b, second], rx1.at[b], rs_sem.at[1, b], rr_sem.at[1, b], (ctx, second * 2 + core)
        )
        d_copies[b].start()
    for b in order:
        first = right if b < half else left
        o_copies[b].wait_recv()
        cs[b] = (pb[b, first].astype(F32) + rxo[b].astype(F32)).astype(BF16)
        c_copies[b] = remote(
            cs.at[b], rx2.at[b], rs_sem.at[2, b], rr_sem.at[2, b], (ctx, first * 2 + core)
        )
        c_copies[b].start()
    for b in order:
        d_copies[b].wait_recv()
        c_copies[b].wait_recv()
        total = pb[b, y].astype(F32) + rx1[b].astype(F32) + rx2[b].astype(F32)
        out_ref[:, pl.ds(b * BLK, BLK)] = total.astype(BF16)

    for i in range(RCH):
        @pl.when(z < nz - 1)
        def _():
            z_copy(i).wait_send()

    for copy in e_copies:
        copy.wait_send()
    for b in order:
        o_copies[b].wait_send()
        d_copies[b].wait_send()
        c_copies[b].wait_send()


def body(nz, projected, conv_weight, log_decay, write_rate, doc_bounds, out_gate, norm_gain, out_weight):
    v = pltpu.VMEM
    dma = pltpu.SemaphoreType.DMA
    vspec = pl.BlockSpec(memory_space=pltpu.VMEM)
    aspec = pl.BlockSpec(memory_space=pl.ANY)
    scratch = [
        v((3, 256, 512), BF16), v((3, 16, 512), BF16), v((3, 136, 512), F32), v((256, 512), BF16),
        v((512, 4096), BF16), v((512, 4096), BF16),
        v((128, 128), F32), v((128, 128), F32), v((6, 128, 128), BF16),
        v((NP, 256, 128), BF16), v((NP, 256, 128), BF16), v((8, 128), F32),
        v((NP, 128, 128), BF16), v((NP, 128, 128), BF16), v((NP, 128, 128), BF16), v((NP, 128, 128), BF16),
        v((NP, 256, 128), BF16), v((NP, 256, 128), BF16),
        v((HEADS, 256, 128), BF16), v((HEADS, 128, 128), BF16), v((HEADS, 128, 128), F32),
        v((HEADS, 256, 128), BF16), v((NX, 256, 128), BF16),
        v((NX, 128, 128), BF16), v((NX, 128, 128), F32), v((128, 128), BF16), v((128, 128), F32),
        v((128, 128), BF16), v((128, 128), BF16), v((NX - 1, 128, 128), BF16), v((NX, 128, 128), BF16),
        v((HEADS, 256, 128), BF16), v((HEADS, 256, 128), F32), v((HEADS, 256, 128), F32),
        v((2, 128, 512), BF16), v((128, 512), BF16), v((128, 4096), F32),
        v((NBLK, NY, 32, BLK), BF16), v((NBLK, 32, BLK), BF16), v((NBLK, 32, BLK), BF16),
        v((NBLK, 32, BLK), BF16), v((NBLK, 32, BLK), BF16),
        dma((3,)), dma((2,)), dma((2,)), dma((3,)), dma((3,)), dma((RCH,)), dma((RCH,)),
        dma((3,)), dma((3,)), dma((4,)), dma((4,)), dma((3, NBLK)), dma((3, NBLK)),
    ]
    return pl.pallas_call(
        functools.partial(kernel, nz),
        out_shape=jax.ShapeDtypeStruct((32, 4096), BF16),
        in_specs=[aspec, vspec, vspec, vspec, pl.BlockSpec(memory_space=pltpu.SMEM), aspec, vspec, aspec],
        out_specs=vspec,
        scratch_shapes=scratch,
        compiler_params=pltpu.CompilerParams(
            collective_id=0, has_side_effects=True, vmem_limit_bytes=56 * 1024 * 1024
        ),
    )(
        projected, conv_weight, log_decay, write_rate, doc_bounds, out_gate,
        norm_gain.reshape(1, -1), out_weight,
    )


def solution(mesh):
    in_specs = (
        P(None, "ctx", "tp"),
        P(None, None, "tp"),
        P("tp", "ctx"),
        P("tp", "ctx"),
        P(),
        P("ctx", "tp"),
        P(),
        P("tp", None),
    )
    out_specs = P(("ctx", "tp"), None)
    nz = mesh.shape["ctx"] // NX
    return jax.shard_map(
        functools.partial(body, nz), mesh=mesh, in_specs=in_specs, out_specs=out_specs, check_vma=False
    )
```

time: 467 us -> 61.5 us (0.13)
  the two profiles are of different devices: /device:TPU:226 before, /device:TPU:224 now
where the time goes in v1:
time: 61.5 us; the launch traced here: 61.3 us
  Pallas kernels  58.3 us (95%)
  local copies, waits for them, and re-layouts  3.01 us (5%)
    pallas_call x1, Pallas kernels, body(): pl.pallas_call(functools.partial(kernel, nz), out_shape=jax.ShapeDtypeStr...  58.3 us
    unnamed x2, local copies, waits for them, and re-layouts  3.01 us

profile of v1, /device:TPU:224, one launch (start us, length us, event | category | flops | bytes accessed | tf_op | source)
XLA Modules:
  0.0 61.3 jit_solution(4967867823207802364)
XLA Ops:
  0.0 1.3 %copy.9.db_ref = s32[8,2]{1,0:T(8,128)} copy(s32[8,2]{0,1:T(2,128)} %param.12) | data formatting | bytes 128 | tf_op args[4]
  1.3 58.3 %shard_map.82 = bf16[32,4096]{1,0:T(8,128)(2,1)} custom-call(bf16[3,256,512]{2,1,0:T(8,128)(2,1)} %proj_hbm.1, f32[3,4,512]{2,1,0:T(4,128)} %cw_ref.1, f32[4,256]{1,0:T(4,128)} %ld_ref.1, f32[4,256]{1,0:T(4,128)} %wr_ref.1, s32[8,2]{1,0:T(8,128)} %copy.9.db_ref, bf16[256,512]{1,0:T(8,128)(2,1)} %gate_hbm.1, f32[1,128]{1,0:T(1,128)} %bitcast.1, ...), custom_call_target="tpu_custom_call" | custom-call | tf_op jit(solution)/shard_map/pallas_call | solution.py:363
  59.7 1.7 %copy.11 = bf16[32,4096]{1,0:T(8,128)(2,1)} copy(bf16[32,4096]{1,0:T(8,128)(2,1)} %shard_map.82) | data formatting | bytes 524288

commit v2 on v1

--- a/solution.py
+++ b/solution.py
@@ -18,7 +18,9 @@
 NP = 8
 BLK = 512
 NBLK = 8
-RCH = 2
+RCH = 4
+PCH = 4
+LOW = 3
 
 
 def mm(a, b):
@@ -34,12 +36,13 @@
 
 
 def kernel(
-    nz, proj_hbm, cw_ref, ld_ref, wr_ref, db_ref, gate_hbm, gain_ref, w_hbm, out_ref,
+    nz, proj_hbm, cw_hbm, ld_hbm, wr_hbm, db_hbm, gate_hbm, gain_hbm, w_hbm, own_out, rx1, rx2,
+    cw_ref, ld_ref, wr_ref, db_ref, gain_ref,
     proj, halo, ext, gate, w_own, w_par,
     gbuf, cbuf, masks, kq, rt, vtmp, lb, pb_s, xb, yb, wub, wts, t1o1, t2, o2, tos, tin,
-    pt, po, rowt, rowo, srx, snd, es, ein, qfin, lfin, sg,
-    nb, nrx, acc, pb, rxo, rx1, rx2, cs,
-    lsem, hsem, wsem, xs_sem, xr_sem, zs_sem, zr_sem, es_sem, er_sem, ns_sem, nr_sem, rs_sem, rr_sem,
+    pt, po, qt, qo, rowt, rowo, prx, psnd, srx, snd, es, ein, qfin, lfin, sg,
+    nb, nrx, acc, pb, rxo, cs,
+    lsem, hsem, wsem, xs_sem, xr_sem, zs_sem, zr_sem, ps_sem, pr_sem, rdy, fsem, es_sem, er_sem, ns_sem, nr_sem, rs_sem, rr_sem,
 ):
     ctx = lax.axis_index("ctx")
     tp = lax.axis_index("tp")
@@ -74,6 +77,15 @@
         pltpu.make_async_copy(gate_hbm, gate, lsem.at[1]),
         pltpu.make_async_copy(w_hbm, w_own, lsem.at[2]),
     ]
+    small = [
+        pltpu.make_async_copy(ld_hbm, ld_ref, lsem.at[3]),
+        pltpu.make_async_copy(wr_hbm, wr_ref, lsem.at[4]),
+        pltpu.make_async_copy(db_hbm, db_ref, lsem.at[5]),
+        pltpu.make_async_copy(cw_hbm, cw_ref, lsem.at[6]),
+        pltpu.make_async_copy(gain_hbm, gain_ref, lsem.at[7]),
+    ]
+    for copy in small:
+        copy.start()
     loads[0].start()
 
     pl.semaphore_wait(barrier, len(peers))
@@ -84,6 +96,17 @@
     loads[2].start()
     w_copy = remote(w_hbm, w_par, wsem.at[0], wsem.at[1], (ctx, y * 2 + other))
     w_copy.start()
+
+    @pl.when(z == LOW + 1)
+    def _():
+        pl.semaphore_signal(rdy, inc=1, device_id=(zdn * NX + x, tp), device_id_type=MESH)
+
+    @pl.when(z == nz - 1)
+    def _():
+        pl.semaphore_signal(rdy, inc=1, device_id=(zup * NX + x, tp), device_id_type=MESH)
+
+    for copy in small:
+        copy.wait()
 
     gbuf[...] = jnp.zeros((128, 128), F32)
     gbuf[0:4, :] = ld_ref[:, 0:128]
@@ -110,8 +133,8 @@
     keeps = []
     for span in range(2):
         hit = jnp.int32(0)
-        for d in range(db_ref.shape[0]):
-            hit = hit + jnp.where(db_ref[d, 0] == ctx * 2 + span, 1, 0)
+        for d in range(db_ref.shape[1]):
+            hit = hit + jnp.where(db_ref[0, d] == ctx * 2 + span, 1, 0)
         keeps.append(1.0 - jnp.minimum(hit, 1).astype(F32))
 
     ones = jnp.full((128, 128), 1.0, BF16)
@@ -190,12 +213,17 @@
         tos[h, 128:256, :] = (d[128:256] + o2[h]).astype(BF16)
 
     x_copies = []
-    for r in range(1, NX):
+    for r in (2, 1, 3):
         to_x = lax.rem(x + r, NX)
         copy = remote(tos.at[to_x], tin.at[x], xs_sem.at[r - 1], xr_sem.at[r - 1], (z * NX + to_x, tp))
         copy.start()
         x_copies.append(copy)
     tin[x] = tos[x]
+
+    @pl.when(z == LOW)
+    def _():
+        pl.semaphore_wait(rdy, 1)
+        pl.semaphore_signal(rdy, inc=1, device_id=(zdn * NX + x, tp), device_id_type=MESH)
 
     for h in range(HEADS):
         for span in range(2):
@@ -235,42 +263,94 @@
             rowo[...] = off
 
     crows = 128 // RCH
-
-    def z_copy(i):
+    prows = 256 // PCH
+
+    def s_copy(i, to, k):
         part = pl.ds(i * crows, crows)
-        return remote(snd.at[part, :], srx.at[part, :], zs_sem.at[i], zr_sem.at[i], (zup * NX + x, tp))
+        return remote(snd.at[part, :], srx.at[part, :], zs_sem.at[i, k], zr_sem.at[i], (to * NX + x, tp))
+
+    def p_copy(i):
+        part = pl.ds(i * prows, prows)
+        return remote(psnd.at[part, :], prx.at[part, :], ps_sem.at[i], pr_sem.at[i], (zup * NX + x, tp))
 
     @pl.when(z == 0)
     def _():
+        snd[...] = rowo[...].astype(BF16)
+        pl.semaphore_wait(rdy, 1)
+        for i in range(RCH):
+            s_copy(i, zup, 0).start()
         srx[...] = jnp.zeros((128, 128), BF16)
 
+    @pl.when(z == LOW)
+    def _():
+        psnd[0:128, :] = rowt[...]
+        psnd[128:256, :] = rowo[...].astype(BF16)
+        for i in range(PCH):
+            p_copy(i).start()
+
+    @pl.when(z <= LOW)
+    def _():
+        prx[0:128, :] = eye_f.astype(BF16)
+        prx[128:256, :] = jnp.zeros((128, 128), BF16)
+
+    @pl.when(z > LOW)
+    def _():
+        for i in range(PCH):
+            part = pl.ds(i * prows, prows)
+            p_copy(i).wait_recv()
+
+            @pl.when(z < nz - 1)
+            def _():
+                new = mm(prx[part, :], rowt[...])
+                if i * prows >= 128:
+                    new = new + rowo[i * prows - 128 : (i + 1) * prows - 128, :]
+                psnd[part, :] = new.astype(BF16)
+                p_copy(i).start()
+
+    for j in range(NX):
+        new = mm(prx[...], pt[j])
+        qt[j] = new[0:128].astype(BF16)
+        qo[j] = new[128:256] + po[j]
+
+    @pl.when(z == LOW - 1)
+    def _():
+        pl.semaphore_wait(rdy, 1)
+
     for i in range(RCH):
+        part = pl.ds(i * crows, crows)
+
         @pl.when(z > 0)
         def _():
-            z_copy(i).wait_recv()
-
-        part = pl.ds(i * crows, crows)
-        snd[part, :] = (mm(srx[part, :], rowt[...]) + rowo[part, :]).astype(BF16)
-
-        @pl.when(z < nz - 1)
+            s_copy(i, zup, 0).wait_recv()
+
+        @pl.when((z > 0) & (z < LOW))
         def _():
-            z_copy(i).start()
-
-    e_copies = []
-    for r in range(1, NX):
+            snd[part, :] = (mm(srx[part, :], rowt[...]) + rowo[part, :]).astype(BF16)
+
+        @pl.when((z > 0) & (z < LOW - 1))
+        def _():
+            s_copy(i, zup, 0).start()
+
+        @pl.when(z == LOW - 1)
+        def _():
+            for far in range(nz - 1, LOW - 1, -1):
+                s_copy(i, far, far - LOW).start()
+
+    e_copies = {}
+    for r in (2, 1, 3):
         to_x = lax.rem(x + r, NX)
-        es[r - 1] = (mm(srx[...], pt[to_x]) + po[to_x]).astype(BF16)
+        es[r - 1] = (mm(srx[...], qt[to_x]) + qo[to_x]).astype(BF16)
         copy = remote(es.at[r - 1], ein.at[x], es_sem.at[r - 1], er_sem.at[r - 1], (z * NX + to_x, tp))
         copy.start()
-        e_copies.append(copy)
-    ein[x] = (mm(srx[...], pt[x]) + po[x]).astype(BF16)
+        e_copies[r] = copy
+    ein[x] = (mm(srx[...], qt[x]) + qo[x]).astype(BF16)
 
     mean_ones = jnp.full((128, 128), 1.0 / 128.0, BF16)
     n_copies = []
-    for r in range(NX):
+    for r in (0, 1, 3, 2):
         head = lax.rem(x + NX - r, NX)
         if r > 0:
-            e_copies[r - 1].wait_recv()
+            e_copies[r].wait_recv()
         att = mmt(qfin[head], ein[head]) + lfin[head]
         ms = mm((att * att).astype(BF16), mean_ones)
         nrm = (att * lax.rsqrt(ms + 1e-05) * sg[head]).astype(BF16)
@@ -295,7 +375,7 @@
 
     order = (0, 4, 1, 5, 2, 6, 3, 7)
     half = NBLK // 2
-    o_copies, d_copies, c_copies = {}, {}, {}
+    o_copies, d_copies, c_copies, f_copies = {}, {}, {}, []
     for b in order:
         cols = pl.ds(b * BLK, BLK)
         res = (acc[:, cols] + mm(nrx[...], w_par[:, cols])).astype(BF16)
@@ -307,29 +387,44 @@
         )
         o_copies[b].start()
         d_copies[b] = remote(
-            pb.at[b, second], rx1.at[b], rs_sem.at[1, b], rr_sem.at[1, b], (ctx, second * 2 + core)
+            pb.at[b, second], rx1.at[:, cols], rs_sem.at[1, b], rr_sem.at[1, b], (ctx, second * 2 + core)
         )
         d_copies[b].start()
+        f_copies.append(pltpu.make_async_copy(pb.at[b, y], own_out.at[:, cols], fsem.at[b]))
+        f_copies[-1].start()
     for b in order:
         first = right if b < half else left
+        cols = pl.ds(b * BLK, BLK)
         o_copies[b].wait_recv()
         cs[b] = (pb[b, first].astype(F32) + rxo[b].astype(F32)).astype(BF16)
         c_copies[b] = remote(
-            cs.at[b], rx2.at[b], rs_sem.at[2, b], rr_sem.at[2, b], (ctx, first * 2 + core)
+            cs.at[b], rx2.at[:, cols], rs_sem.at[2, b], rr_sem.at[2, b], (ctx, first * 2 + core)
         )
         c_copies[b].start()
     for b in order:
         d_copies[b].wait_recv()
         c_copies[b].wait_recv()
-        total = pb[b, y].astype(F32) + rx1[b].astype(F32) + rx2[b].astype(F32)
-        out_ref[:, pl.ds(b * BLK, BLK)] = total.astype(BF16)
-
-    for i in range(RCH):
-        @pl.when(z < nz - 1)
-        def _():
-            z_copy(i).wait_send()
-
-    for copy in e_copies:
+
+    for copy in f_copies:
+        copy.wait()
+
+    @pl.when(z < LOW - 1)
+    def _():
+        for i in range(RCH):
+            s_copy(i, zup, 0).wait_send()
+
+    @pl.when(z == LOW - 1)
+    def _():
+        for i in range(RCH):
+            for far in range(LOW, nz):
+                s_copy(i, far, far - LOW).wait_send()
+
+    @pl.when((z >= LOW) & (z < nz - 1))
+    def _():
+        for i in range(PCH):
+            p_copy(i).wait_send()
+
+    for copy in e_copies.values():
         copy.wait_send()
     for b in order:
         o_copies[b].wait_send()
@@ -343,6 +438,8 @@
     vspec = pl.BlockSpec(memory_space=pltpu.VMEM)
     aspec = pl.BlockSpec(memory_space=pl.ANY)
     scratch = [
+        v((3, TAPS, 512), F32), v((HEADS, 256), F32), v((HEADS, 256), F32),
+        pltpu.SMEM((2, 8), jnp.int32), v((1, 128), F32),
         v((3, 256, 512), BF16), v((3, 16, 512), BF16), v((3, 136, 512), F32), v((256, 512), BF16),
         v((512, 4096), BF16), v((512, 4096), BF16),
         v((128, 128), F32), v((128, 128), F32), v((6, 128, 128), BF16),
@@ -351,28 +448,31 @@
         v((NP, 256, 128), BF16), v((NP, 256, 128), BF16),
         v((HEADS, 256, 128), BF16), v((HEADS, 128, 128), BF16), v((HEADS, 128, 128), F32),
         v((HEADS, 256, 128), BF16), v((NX, 256, 128), BF16),
-        v((NX, 128, 128), BF16), v((NX, 128, 128), F32), v((128, 128), BF16), v((128, 128), F32),
+        v((NX, 128, 128), BF16), v((NX, 128, 128), F32), v((NX, 128, 128), BF16), v((NX, 128, 128), F32),
+        v((128, 128), BF16), v((128, 128), F32), v((256, 128), BF16), v((256, 128), BF16),
         v((128, 128), BF16), v((128, 128), BF16), v((NX - 1, 128, 128), BF16), v((NX, 128, 128), BF16),
         v((HEADS, 256, 128), BF16), v((HEADS, 256, 128), F32), v((HEADS, 256, 128), F32),
         v((2, 128, 512), BF16), v((128, 512), BF16), v((128, 4096), F32),
         v((NBLK, NY, 32, BLK), BF16), v((NBLK, 32, BLK), BF16), v((NBLK, 32, BLK), BF16),
-        v((NBLK, 32, BLK), BF16), v((NBLK, 32, BLK), BF16),
-        dma((3,)), dma((2,)), dma((2,)), dma((3,)), dma((3,)), dma((RCH,)), dma((RCH,)),
+        dma((8,)), dma((2,)), dma((2,)), dma((3,)), dma((3,)), dma((RCH, nz - LOW)), dma((RCH,)),
+        dma((PCH,)), dma((PCH,)), pltpu.SemaphoreType.REGULAR, dma((NBLK,)),
         dma((3,)), dma((3,)), dma((4,)), dma((4,)), dma((3, NBLK)), dma((3, NBLK)),
     ]
-    return pl.pallas_call(
+    half = jax.ShapeDtypeStruct((32, 4096), BF16)
+    own, one, two = pl.pallas_call(
         functools.partial(kernel, nz),
-        out_shape=jax.ShapeDtypeStruct((32, 4096), BF16),
-        in_specs=[aspec, vspec, vspec, vspec, pl.BlockSpec(memory_space=pltpu.SMEM), aspec, vspec, aspec],
-        out_specs=vspec,
+        out_shape=(half, half, half),
+        in_specs=[aspec] * 8,
+        out_specs=(aspec, aspec, aspec),
         scratch_shapes=scratch,
         compiler_params=pltpu.CompilerParams(
             collective_id=0, has_side_effects=True, vmem_limit_bytes=56 * 1024 * 1024
         ),
     )(
-        projected, conv_weight, log_decay, write_rate, doc_bounds, out_gate,
+        projected, conv_weight, log_decay, write_rate, doc_bounds.T, out_gate,
         norm_gain.reshape(1, -1), out_weight,
     )
+    return (own.astype(F32) + one.astype(F32) + two.astype(F32)).astype(BF16)
 
 
 def solution(mesh):

time: 61.5 us -> 48.7 us (0.79)
  the two profiles are of different devices: /device:TPU:224 before, /device:TPU:226 now
where the time goes in v2:
time: 48.7 us; the launch traced here: 48.4 us
  Pallas kernels  46.5 us (95%)
  other arithmetic  1.91 us (4%)
    pallas_call x1, Pallas kernels, body(): pl.pallas_call(functools.partial(kernel, nz), out_shape=(half, half, half...  46.5 us
    convert_element_type x1, other arithmetic, body(): return (own.astype(F32) + one.astype(F32) + two.astype(F32)).astype(BF16)  1.91 us

profile of v2, /device:TPU:226, one launch (start us, length us, event | category | flops | bytes accessed | tf_op | source)
XLA Modules:
  0.0 48.4 jit_solution(12400446797401269514)
XLA Ops:
  0.0 46.5 %shard_map.82 = (bf16[32,4096]{1,0:T(8,128)(2,1)}, bf16[32,4096]{1,0:T(8,128)(2,1)}, bf16[32,4096]{1,0:T(8,128)(2,1)}) custom-call(bf16[3,256,512]{2,1,0:T(8,128)(2,1)} %proj_hbm.1, f32[3,4,512]{2,1,0:T(4,128)} %cw_hbm.1, f32[4,256]{1,0:T(4,128)} %ld_hbm.1, f32[4,256]{1,0:T(4,128)} %wr_hbm.1, s32[2,8]{1,0:T(2,128)} %bitcast.2, bf16[256,512]{1,0:T(8,128)(2,1)} %gate_hbm.1, ...), custom_call_target="tpu_custom_call" | custom-call | tf_op jit(solution)/shard_map/pallas_call | solution.py:462
  46.5 1.9 %add_convert_fusion = bf16[32,4096]{1,0:T(8,128)(2,1)} fusion(bf16[32,4096]{1,0:T(8,128)(2,1)} %get-tuple-element.10, bf16[32,4096]{1,0:T(8,128)(2,1)} %get-tuple-element.9, bf16[32,4096]{1,0:T(8,128)(2,1)} %get-tuple-element.8), kind=kLoop, calls=%fused_computation | loop fusion | flops 786432 | bytes 1048576 | tf_op jit(solution)/shard_map/convert_element_type | solution.py:475

commit v3 on v2

--- a/solution.py
+++ b/solution.py
@@ -20,6 +20,7 @@
 NBLK = 8
 RCH = 4
 PCH = 4
+HEAD = 4
 LOW = 3
 
 
@@ -39,7 +40,7 @@
     nz, proj_hbm, cw_hbm, ld_hbm, wr_hbm, db_hbm, gate_hbm, gain_hbm, w_hbm, own_out, rx1, rx2,
     cw_ref, ld_ref, wr_ref, db_ref, gain_ref,
     proj, halo, ext, gate, w_own, w_par,
-    gbuf, cbuf, masks, kq, rt, vtmp, lb, pb_s, xb, yb, wub, wts, t1o1, t2, o2, tos, tin,
+    gbuf, cbuf, masks, kq, rt, vb, lb, pb_s, xb, yb, xc, wub, wts, t1o1, t2, o2, tos, tin,
     pt, po, qt, qo, rowt, rowo, prx, psnd, srx, snd, es, ein, qfin, lfin, sg,
     nb, nrx, acc, pb, rxo, cs,
     lsem, hsem, wsem, xs_sem, xr_sem, zs_sem, zr_sem, ps_sem, pr_sem, rdy, fsem, es_sem, er_sem, ns_sem, nr_sem, rs_sem, rr_sem,
@@ -88,6 +89,16 @@
         copy.start()
     loads[0].start()
 
+    row_i = lax.broadcasted_iota(jnp.int32, (128, 128), 0)
+    col_i = lax.broadcasted_iota(jnp.int32, (128, 128), 1)
+    eye = row_i == col_i
+    eye_f = jnp.where(eye, 1.0, 0.0)
+    for level in range(1, 7):
+        low = lax.shift_right_logical(row_i, level)
+        low_j = lax.shift_right_logical(col_i, level)
+        same = lax.shift_right_logical(row_i, level + 1) == lax.shift_right_logical(col_i, level + 1)
+        masks[level - 1] = jnp.where(same & (low > low_j), 1.0, 0.0).astype(BF16)
+
     pl.semaphore_wait(barrier, len(peers))
     rows = proj_hbm.shape[1]
     halo_copy = remote(proj_hbm.at[:, pl.ds(rows - 16, 16), :], halo, hsem.at[0], hsem.at[1], (nxt, tp))
@@ -120,16 +131,6 @@
     gbuf[0:8, :] = run
     cbuf[...] = gbuf[...].T
 
-    row_i = lax.broadcasted_iota(jnp.int32, (128, 128), 0)
-    col_i = lax.broadcasted_iota(jnp.int32, (128, 128), 1)
-    eye = row_i == col_i
-    eye_f = jnp.where(eye, 1.0, 0.0)
-    for level in range(1, 7):
-        low = lax.shift_right_logical(row_i, level)
-        low_j = lax.shift_right_logical(col_i, level)
-        same = lax.shift_right_logical(row_i, level + 1) == lax.shift_right_logical(col_i, level + 1)
-        masks[level - 1] = jnp.where(same & (low > low_j), 1.0, 0.0).astype(BF16)
-
     keeps = []
     for span in range(2):
         hit = jnp.int32(0)
@@ -139,74 +140,126 @@
 
     ones = jnp.full((128, 128), 1.0, BF16)
 
-    def conv_span(span):
-        base = span * SPAN
-        for s in (1, 2, 0):
-            if span == 0:
-                before = halo[s, 8:16, :].astype(F32)
-            else:
-                before = proj[s, base - 8 : base, :].astype(F32)
-            ext[s, 0:8, :] = before * keeps[span]
-            ext[s, 8:136, :] = proj[s, base : base + SPAN, :].astype(F32)
+    def activate(s, h, first, count):
+        cols = pl.ds(h * 128, 128)
+        u = cw_ref[s, 0:1, cols] * ext[s, 8 + first : 8 + first + count, cols]
+        for j in range(1, TAPS):
+            lo = 8 + first - j
+            u = u + cw_ref[s, j : j + 1, cols] * ext[s, lo : lo + count, cols]
+        return silu(u)
+
+    def unit(a):
+        ss = mm((a * a).astype(BF16), ones)
+        return (a * lax.rsqrt(ss + 1e-06)).astype(BF16)
+
+    def fill(streams, span, first, count):
+        for s in streams:
             for h in range(HEADS):
                 p = span * HEADS + h
-                cols = pl.ds(h * 128, 128)
-                u = cw_ref[s, 0:1, cols] * ext[s, 8:136, cols]
-                for j in range(1, TAPS):
-                    u = u + cw_ref[s, j : j + 1, cols] * ext[s, 8 - j : 136 - j, cols]
-                a = silu(u)
-                if s == 2:
-                    rt[p, 128:256, :] = (a.T * gbuf[8 + p : 9 + p, :]).astype(BF16)
+                a = activate(s, h, first, count)
+                if s == 1:
+                    kq[p, first : first + count, :] = unit(a)
+                elif s == 0:
+                    kq[p, 128 + first : 128 + first + count, :] = unit(a)
                 else:
-                    ss = mm((a * a).astype(BF16), ones)
-                    n = a * lax.rsqrt(ss + 1e-06)
-                    nbf = n.astype(BF16)
-                    if s == 1:
-                        kq[p, 0:128, :] = nbf
-                        scale = gbuf[8 + p : 9 + p, :] * jnp.exp(gbuf[p : p + 1, :])
-                        rt[p, 0:128, :] = (nbf.astype(F32).T * scale).astype(BF16)
-                    else:
-                        kq[p, 128:256, :] = nbf
-
-    def scores(p):
-        a = mmt(kq[p], kq[p, 0:128, :])
+                    vb[p, first : first + count, :] = a.astype(BF16)
+
+    def transposed(p):
+        beta = gbuf[8 + p : 9 + p, :]
+        scale = beta * jnp.exp(gbuf[p : p + 1, :])
+        rt[p, 0:128, :] = (kq[p, 0:128, :].astype(F32).T * scale).astype(BF16)
+        rt[p, 128:256, :] = (vb[p].astype(F32).T * beta).astype(BF16)
+
+    def decays(p):
         gcol = jnp.broadcast_to(cbuf[:, p : p + 1], (128, 128))
         bcol = jnp.broadcast_to(cbuf[:, 8 + p : 9 + p], (128, 128))
         dm = jnp.exp(jnp.minimum(gcol - gbuf[p : p + 1, :], 0.0))
-        low = jnp.where(row_i > col_i, bcol * dm * a[0:128], 0.0)
+        return dm, bcol * dm
+
+    def scores(p):
+        a = mmt(kq[p, 0:128, :], kq[p, 0:128, :])
+        return jnp.where(row_i > col_i, decays(p)[1] * a, 0.0)
+
+    def pairs(low):
+        pair = lax.shift_right_logical(row_i, 1) == lax.shift_right_logical(col_i, 1)
+        return (eye_f - jnp.where(pair, low, 0.0)).astype(BF16)
+
+    def updates(p):
+        wu = mmt(rt[p], xb[p])
+        wub[p] = wu.astype(BF16)
+        g = gbuf[p : p + 1, :]
+        wts[p] = (wu * jnp.exp(g[:, 127:128] - g)).astype(BF16)
+
+    def maps(p):
+        span, h = p // HEADS, p % HEADS
+        to = mm(wts[p], kq[p, 0:128, :])
+        last = jnp.exp(gbuf[p : p + 1, 127:128])
+        t = keeps[span] * (last * eye_f - to[0:128])
+        if span == 0:
+            t1o1[h, 0:128, :] = t.astype(BF16)
+            t1o1[h, 128:256, :] = to[128:256].astype(BF16)
+        else:
+            t2[h] = t.astype(BF16)
+            o2[h] = to[128:256]
+
+    first_span = range(HEADS)
+    second_span = range(HEADS, NP)
+
+    loads[0].wait()
+    for span in (1, 0):
+        for s in (1, 2):
+            if span == 0:
+                ext[s, 0:8, :] = jnp.zeros((8, 512), F32)
+            else:
+                ext[s, 0:8, :] = proj[s, SPAN - 8 : SPAN, :].astype(F32) * keeps[1]
+            ext[s, 8:136, :] = proj[s, span * SPAN : span * SPAN + SPAN, :].astype(F32)
+        fill((1, 2), span, 0, SPAN)
+    for p in second_span:
+        low = scores(p)
         lb[p] = low.astype(BF16)
-        pb_s[p] = jnp.where(row_i >= col_i, dm * a[128:256], 0.0).astype(BF16)
-        pair = lax.shift_right_logical(row_i, 1) == lax.shift_right_logical(col_i, 1)
-        xb[p] = (eye_f - jnp.where(pair, low, 0.0)).astype(BF16)
-
-    loads[0].wait()
-    conv_span(1)
-    halo_copy.wait()
-    conv_span(0)
-    for p in range(NP):
-        scores(p)
+        xb[p] = pairs(low)
+    for p in first_span:
+        low = jnp.where(col_i >= HEAD, scores(p), 0.0)
+        lb[p] = low.astype(BF16)
+        xb[p] = pairs(low)
+    for p in second_span:
+        transposed(p)
     for level in range(1, 7):
         for p in range(NP):
             yb[p] = mm(xb[p], lb[p] * masks[level - 1]).astype(BF16)
         for p in range(NP):
             xb[p] = xb[p] - mm(yb[p], xb[p]).astype(BF16)
-    for p in range(NP):
-        wu = mmt(rt[p], xb[p])
-        wub[p] = wu.astype(BF16)
-        g = gbuf[p : p + 1, :]
-        wts[p] = (wu * jnp.exp(g[:, 127:128] - g)).astype(BF16)
-    for h in range(HEADS):
-        for span in range(2):
-            p = span * HEADS + h
-            to = mm(wts[p], kq[p, 0:128, :])
-            last = jnp.exp(gbuf[p : p + 1, 127:128])
-            t = keeps[span] * (last * eye_f - to[0:128])
-            if span == 0:
-                t1o1[h, 0:128, :] = t.astype(BF16)
-                t1o1[h, 128:256, :] = to[128:256].astype(BF16)
-            else:
-                t2[h] = t.astype(BF16)
-                o2[h] = to[128:256]
+    for p in second_span:
+        updates(p)
+    for p in second_span:
+        maps(p)
+
+    halo_copy.wait()
+    for s in (1, 2):
+        ext[s, 0:8, :] = halo[s, 8:16, :].astype(F32) * keeps[0]
+    fill((1, 2), 0, 0, 16)
+    corner = (row_i < HEAD) & (col_i < HEAD)
+    below = (row_i >= HEAD) & (col_i < HEAD)
+    for p in first_span:
+        low = scores(p)
+        lb[p] = jnp.where(below, low, 0.0).astype(BF16)
+        low = jnp.where(corner, low, 0.0)
+        yb[p] = low.astype(BF16)
+        xc[p] = pairs(low)
+    for p in first_span:
+        transposed(p)
+    for p in first_span:
+        yb[p] = mm(xc[p], yb[p] * masks[0]).astype(BF16)
+    for p in first_span:
+        xb[p] = xb[p] + (xc[p] - eye_f.astype(BF16) - mm(yb[p], xc[p]).astype(BF16))
+    for p in first_span:
+        yb[p] = mm(xb[p], lb[p]).astype(BF16)
+    for p in first_span:
+        xb[p] = xb[p] - mm(yb[p], xb[p]).astype(BF16)
+    for p in first_span:
+        updates(p)
+    for p in first_span:
+        maps(p)
     for h in range(HEADS):
         d = mm(t1o1[h], t2[h])
         tos[h, 0:128, :] = d[0:128].astype(BF16)
@@ -225,6 +278,14 @@
         pl.semaphore_wait(rdy, 1)
         pl.semaphore_signal(rdy, inc=1, device_id=(zdn * NX + x, tp), device_id_type=MESH)
 
+    for span in range(2):
+        before = halo[0, 8:16, :] if span == 0 else proj[0, SPAN - 8 : SPAN, :]
+        ext[0, 0:8, :] = before.astype(F32) * keeps[span]
+        ext[0, 8:136, :] = proj[0, span * SPAN : span * SPAN + SPAN, :].astype(F32)
+        fill((0,), span, 0, SPAN)
+    for p in range(NP):
+        a = mmt(kq[p, 128:256, :], kq[p, 0:128, :])
+        pb_s[p] = jnp.where(row_i >= col_i, decays(p)[0] * a, 0.0).astype(BF16)
     for h in range(HEADS):
         for span in range(2):
             p = span * HEADS + h
@@ -443,8 +504,9 @@
         v((3, 256, 512), BF16), v((3, 16, 512), BF16), v((3, 136, 512), F32), v((256, 512), BF16),
         v((512, 4096), BF16), v((512, 4096), BF16),
         v((128, 128), F32), v((128, 128), F32), v((6, 128, 128), BF16),
-        v((NP, 256, 128), BF16), v((NP, 256, 128), BF16), v((8, 128), F32),
+        v((NP, 256, 128), BF16), v((NP, 256, 128), BF16), v((NP, 128, 128), BF16),
         v((NP, 128, 128), BF16), v((NP, 128, 128), BF16), v((NP, 128, 128), BF16), v((NP, 128, 128), BF16),
+        v((HEADS, 128, 128), BF16),
         v((NP, 256, 128), BF16), v((NP, 256, 128), BF16),
         v((HEADS, 256, 128), BF16), v((HEADS, 128, 128), BF16), v((HEADS, 128, 128), F32),
         v((HEADS, 256, 128), BF16), v((NX, 256, 128), BF16),

time: 48.7 us -> 47.4 us (0.973)
  Pallas kernels: 46.5 us -> 45.4 us
    pallas_call x1, Pallas kernels: 46.5 us -> 45.4 us  [body(): pl.pallas_call(functools.partial(kernel, nz), out_shape=(half, half, half...]
where the time goes in v3:
time: 47.4 us; the launch traced here: 47.3 us
  Pallas kernels  45.4 us (96%)
  other arithmetic  1.91 us (4%)
    pallas_call x1, Pallas kernels, body(): pl.pallas_call(functools.partial(kernel, nz), out_shape=(half, half, half...  45.4 us
    convert_element_type x1, other arithmetic, body(): return (own.astype(F32) + one.astype(F32) + two.astype(F32)).astype(BF16)  1.91 us

profile of v3, /device:TPU:226, one launch (start us, length us, event | category | flops | bytes accessed | tf_op | source)
XLA Modules:
  0.0 47.3 jit_solution(3974374240012864634)
XLA Ops:
  0.0 45.4 %shard_map.82 = (bf16[32,4096]{1,0:T(8,128)(2,1)}, bf16[32,4096]{1,0:T(8,128)(2,1)}, bf16[32,4096]{1,0:T(8,128)(2,1)}) custom-call(bf16[3,256,512]{2,1,0:T(8,128)(2,1)} %proj_hbm.1, f32[3,4,512]{2,1,0:T(4,128)} %cw_hbm.1, f32[4,256]{1,0:T(4,128)} %ld_hbm.1, f32[4,256]{1,0:T(4,128)} %wr_hbm.1, s32[2,8]{1,0:T(2,128)} %bitcast.2, bf16[256,512]{1,0:T(8,128)(2,1)} %gate_hbm.1, ...), custom_call_target="tpu_custom_call" | custom-call | tf_op jit(solution)/shard_map/pallas_call | solution.py:524
  45.4 1.9 %add_convert_fusion = bf16[32,4096]{1,0:T(8,128)(2,1)} fusion(bf16[32,4096]{1,0:T(8,128)(2,1)} %get-tuple-element.10, bf16[32,4096]{1,0:T(8,128)(2,1)} %get-tuple-element.9, bf16[32,4096]{1,0:T(8,128)(2,1)} %get-tuple-element.8), kind=kLoop, calls=%fused_computation | loop fusion | flops 786432 | bytes 1048576 | tf_op jit(solution)/shard_map/convert_element_type | solution.py:537

commit v4 on v3

--- a/solution.py
+++ b/solution.py
@@ -40,10 +40,10 @@
     nz, proj_hbm, cw_hbm, ld_hbm, wr_hbm, db_hbm, gate_hbm, gain_hbm, w_hbm, own_out, rx1, rx2,
     cw_ref, ld_ref, wr_ref, db_ref, gain_ref,
     proj, halo, ext, gate, w_own, w_par,
-    gbuf, cbuf, masks, kq, rt, vb, lb, pb_s, xb, yb, xc, wub, wts, t1o1, t2, o2, tos, tin,
+    gbuf, cbuf, masks, kq, rt, vb, lb, pb_s, xb, yb, xc, wub, wts, t1o1, t2, o2, tos, tin, am, ain, ab, mb,
     pt, po, qt, qo, rowt, rowo, prx, psnd, srx, snd, es, ein, qfin, lfin, sg,
     nb, nrx, acc, pb, rxo, cs,
-    lsem, hsem, wsem, xs_sem, xr_sem, zs_sem, zr_sem, ps_sem, pr_sem, rdy, fsem, es_sem, er_sem, ns_sem, nr_sem, rs_sem, rr_sem,
+    lsem, hsem, wsem, xs_sem, xr_sem, as_sem, ar_sem, zs_sem, zr_sem, ps_sem, pr_sem, rdy, fsem, es_sem, er_sem, ns_sem, nr_sem, rs_sem, rr_sem,
 ):
     ctx = lax.axis_index("ctx")
     tp = lax.axis_index("tp")
@@ -99,23 +99,6 @@
         same = lax.shift_right_logical(row_i, level + 1) == lax.shift_right_logical(col_i, level + 1)
         masks[level - 1] = jnp.where(same & (low > low_j), 1.0, 0.0).astype(BF16)
 
-    pl.semaphore_wait(barrier, len(peers))
-    rows = proj_hbm.shape[1]
-    halo_copy = remote(proj_hbm.at[:, pl.ds(rows - 16, 16), :], halo, hsem.at[0], hsem.at[1], (nxt, tp))
-    halo_copy.start()
-    loads[1].start()
-    loads[2].start()
-    w_copy = remote(w_hbm, w_par, wsem.at[0], wsem.at[1], (ctx, y * 2 + other))
-    w_copy.start()
-
-    @pl.when(z == LOW + 1)
-    def _():
-        pl.semaphore_signal(rdy, inc=1, device_id=(zdn * NX + x, tp), device_id_type=MESH)
-
-    @pl.when(z == nz - 1)
-    def _():
-        pl.semaphore_signal(rdy, inc=1, device_id=(zup * NX + x, tp), device_id_type=MESH)
-
     for copy in small:
         copy.wait()
 
@@ -164,9 +147,13 @@
                 else:
                     vb[p, first : first + count, :] = a.astype(BF16)
 
-    def transposed(p):
+    def transposed(p, skip=0):
         beta = gbuf[8 + p : 9 + p, :]
-        scale = beta * jnp.exp(gbuf[p : p + 1, :])
+        g = gbuf[p : p + 1, :]
+        if skip:
+            g = g - g[:, skip - 1 : skip]
+            beta = jnp.where(col_i[0:1, :] >= skip, beta, 0.0)
+        scale = beta * jnp.exp(g)
         rt[p, 0:128, :] = (kq[p, 0:128, :].astype(F32).T * scale).astype(BF16)
         rt[p, 128:256, :] = (vb[p].astype(F32).T * beta).astype(BF16)
 
@@ -205,6 +192,25 @@
     first_span = range(HEADS)
     second_span = range(HEADS, NP)
 
+    rows = proj_hbm.shape[1]
+    halo_copy = remote(proj_hbm.at[:, pl.ds(rows - 16, 16), :], halo, hsem.at[0], hsem.at[1], (nxt, tp))
+    w_copy = remote(w_hbm, w_par, wsem.at[0], wsem.at[1], (ctx, y * 2 + other))
+
+    def enter():
+        pl.semaphore_wait(barrier, len(peers))
+        halo_copy.start()
+        loads[1].start()
+        loads[2].start()
+        w_copy.start()
+
+        @pl.when(z == LOW + 1)
+        def _():
+            pl.semaphore_signal(rdy, inc=1, device_id=(zdn * NX + x, tp), device_id_type=MESH)
+
+        @pl.when(z == nz - 1)
+        def _():
+            pl.semaphore_signal(rdy, inc=1, device_id=(zup * NX + x, tp), device_id_type=MESH)
+
     loads[0].wait()
     for span in (1, 0):
         for s in (1, 2):
@@ -214,52 +220,32 @@
                 ext[s, 0:8, :] = proj[s, SPAN - 8 : SPAN, :].astype(F32) * keeps[1]
             ext[s, 8:136, :] = proj[s, span * SPAN : span * SPAN + SPAN, :].astype(F32)
         fill((1, 2), span, 0, SPAN)
-    for p in second_span:
+        if span == 1:
+            enter()
+    for p in range(NP):
         low = scores(p)
-        lb[p] = low.astype(BF16)
-        xb[p] = pairs(low)
-    for p in first_span:
-        low = jnp.where(col_i >= HEAD, scores(p), 0.0)
+        if p < HEADS:
+            low = jnp.where(col_i >= HEAD, low, 0.0)
         lb[p] = low.astype(BF16)
         xb[p] = pairs(low)
     for p in second_span:
         transposed(p)
+    for p in first_span:
+        transposed(p, HEAD)
     for level in range(1, 7):
         for p in range(NP):
             yb[p] = mm(xb[p], lb[p] * masks[level - 1]).astype(BF16)
         for p in range(NP):
             xb[p] = xb[p] - mm(yb[p], xb[p]).astype(BF16)
-    for p in second_span:
+    for p in range(NP):
         updates(p)
     for p in second_span:
         maps(p)
-
-    halo_copy.wait()
-    for s in (1, 2):
-        ext[s, 0:8, :] = halo[s, 8:16, :].astype(F32) * keeps[0]
-    fill((1, 2), 0, 0, 16)
-    corner = (row_i < HEAD) & (col_i < HEAD)
-    below = (row_i >= HEAD) & (col_i < HEAD)
-    for p in first_span:
-        low = scores(p)
-        lb[p] = jnp.where(below, low, 0.0).astype(BF16)
-        low = jnp.where(corner, low, 0.0)
-        yb[p] = low.astype(BF16)
-        xc[p] = pairs(low)
-    for p in first_span:
-        transposed(p)
-    for p in first_span:
-        yb[p] = mm(xc[p], yb[p] * masks[0]).astype(BF16)
-    for p in first_span:
-        xb[p] = xb[p] + (xc[p] - eye_f.astype(BF16) - mm(yb[p], xc[p]).astype(BF16))
-    for p in first_span:
-        yb[p] = mm(xb[p], lb[p]).astype(BF16)
-    for p in first_span:
-        xb[p] = xb[p] - mm(yb[p], xb[p]).astype(BF16)
-    for p in first_span:
-        updates(p)
-    for p in first_span:
-        maps(p)
+    for p in first_span:
+        to = mm(wts[p], kq[p, 0:128, :])
+        last = jnp.exp(gbuf[p : p + 1, 127:128] - gbuf[p : p + 1, HEAD - 1 : HEAD])
+        t1o1[p, 0:128, :] = (last * eye_f - to[0:128]).astype(BF16)
+        t1o1[p, 128:256, :] = to[128:256].astype(BF16)
     for h in range(HEADS):
         d = mm(t1o1[h], t2[h])
         tos[h, 0:128, :] = d[0:128].astype(BF16)
@@ -277,6 +263,66 @@
     def _():
         pl.semaphore_wait(rdy, 1)
         pl.semaphore_signal(rdy, inc=1, device_id=(zdn * NX + x, tp), device_id_type=MESH)
+
+    halo_copy.wait()
+    for s in (1, 2):
+        ext[s, 0:8, :] = halo[s, 8:16, :].astype(F32) * keeps[0]
+    fill((1, 2), 0, 0, 16)
+    for h in range(HEADS):
+        keys = kq[h, 0:16, :].astype(F32)
+        gcol = jnp.broadcast_to(cbuf[0:16, h : h + 1], (16, 128))
+        bcol = jnp.broadcast_to(cbuf[0:16, 8 + h : 9 + h], (16, 128))
+        low = bcol * jnp.exp(jnp.minimum(gcol - gbuf[h : h + 1, :], 0.0))
+        low = low * mmt(kq[h, 0:16, :], kq[h, 0:128, :])
+        rk = keys * bcol * jnp.exp(gcol)
+        rv = vb[h, 0:16, :].astype(F32) * bcol
+        ws, us = [], []
+        for i in range(HEAD):
+            w_row, u_row = rk[i : i + 1, :], rv[i : i + 1, :]
+            for j in range(i):
+                c = jnp.broadcast_to(low[i : i + 1, j : j + 1], (1, 128))
+                w_row = w_row - c * ws[j]
+                u_row = u_row - c * us[j]
+            ws.append(w_row)
+            us.append(u_row)
+        end = jnp.broadcast_to(cbuf[HEAD - 1 : HEAD, h : h + 1], (8, 128))
+        am[h] = jnp.zeros((32, 128), F32)
+        for i in range(HEAD):
+            am[h, i : i + 1, :] = -keeps[0] * ws[i]
+            am[h, 8 + i : 9 + i, :] = us[i]
+        tail = jnp.exp(end - gcol[0:8]) * keys[0:8]
+        am[h, 16:24, :] = jnp.where(row_i[0:8] < HEAD, tail, 0.0)
+        am[h, 24:32, :] = keeps[0] * jnp.exp(end)
+    a_copies = []
+    for r in (2, 1, 3):
+        to_x = lax.rem(x + r, NX)
+        copy = remote(am.at[to_x], ain.at[x], as_sem.at[r - 1], ar_sem.at[r - 1], (z * NX + to_x, tp))
+        copy.start()
+        a_copies.append(copy)
+    ain[x] = am[x]
+
+    corner = (row_i < HEAD) & (col_i < HEAD)
+    below = (row_i >= HEAD) & (col_i < HEAD)
+    for p in first_span:
+        low = scores(p)
+        lb[p] = jnp.where(below, low, 0.0).astype(BF16)
+        low = jnp.where(corner, low, 0.0)
+        yb[p] = low.astype(BF16)
+        xc[p] = pairs(low)
+    for p in first_span:
+        transposed(p)
+    for p in first_span:
+        yb[p] = mm(xc[p], yb[p] * masks[0]).astype(BF16)
+    for p in first_span:
+        xb[p] = xb[p] + (xc[p] - eye_f.astype(BF16) - mm(yb[p], xc[p]).astype(BF16))
+    for p in first_span:
+        yb[p] = mm(xb[p], lb[p]).astype(BF16)
+    for p in first_span:
+        xb[p] = xb[p] - mm(yb[p], xb[p]).astype(BF16)
+    for p in first_span:
+        updates(p)
+    for p in first_span:
+        maps(p)
 
     for span in range(2):
         before = halo[0, 8:16, :] if span == 0 else proj[0, SPAN - 8 : SPAN, :]
@@ -306,15 +352,24 @@
 
     for copy in x_copies:
         copy.wait()
-
+    for copy in a_copies:
+        copy.wait()
+
+    for j in range(NX):
+        ab[j] = mm(ain[j, 16:24, :].astype(BF16), tin[j, 0:128, :])
+    for j in range(NX):
+        wu = jnp.concatenate([ain[j, 0:8, :], ain[j, 8:16, :]], axis=1).astype(BF16)
+        low = lax.dot_general(wu, ab[j].astype(BF16), (((0,), (0,)), ((), ())), preferred_element_type=F32)
+        mb[j, 0:128, :] = (tin[j, 0:128, :].astype(F32) * ain[j, 24:25, :] + low[0:128]).astype(BF16)
+        mb[j, 128:256, :] = (tin[j, 128:256, :].astype(F32) + low[128:256]).astype(BF16)
     pt[0] = eye_f.astype(BF16)
     po[0] = jnp.zeros((128, 128), F32)
-    pt[1] = tin[0, 0:128, :]
-    po[1] = tin[0, 128:256, :].astype(F32)
-    cur = tin[0]
+    pt[1] = mb[0, 0:128, :]
+    po[1] = mb[0, 128:256, :].astype(F32)
+    cur = mb[0]
     for j in range(1, NX):
-        step = mm(cur, tin[j, 0:128, :])
-        off = step[128:256] + tin[j, 128:256, :].astype(F32)
+        step = mm(cur, mb[j, 0:128, :])
+        off = step[128:256] + mb[j, 128:256, :].astype(F32)
         if j < NX - 1:
             pt[j + 1] = step[0:128].astype(BF16)
             po[j + 1] = off
@@ -377,6 +432,13 @@
     def _():
         pl.semaphore_wait(rdy, 1)
 
+    def e_copy(r, i, to_x):
+        part = pl.ds(i * crows, crows)
+        return remote(
+            es.at[r - 1, part, :], ein.at[x, part, :], es_sem.at[r - 1, i], er_sem.at[r - 1, i], (z * NX + to_x, tp)
+        )
+
+    e_copies = {}
     for i in range(RCH):
         part = pl.ds(i * crows, crows)
 
@@ -397,21 +459,20 @@
             for far in range(nz - 1, LOW - 1, -1):
                 s_copy(i, far, far - LOW).start()
 
-    e_copies = {}
-    for r in (2, 1, 3):
-        to_x = lax.rem(x + r, NX)
-        es[r - 1] = (mm(srx[...], qt[to_x]) + qo[to_x]).astype(BF16)
-        copy = remote(es.at[r - 1], ein.at[x], es_sem.at[r - 1], er_sem.at[r - 1], (z * NX + to_x, tp))
-        copy.start()
-        e_copies[r] = copy
-    ein[x] = (mm(srx[...], qt[x]) + qo[x]).astype(BF16)
+        for r in (2, 1, 3):
+            to_x = lax.rem(x + r, NX)
+            es[r - 1, part, :] = (mm(srx[part, :], qt[to_x]) + qo[to_x, part, :]).astype(BF16)
+            e_copies[r, i] = e_copy(r, i, to_x)
+            e_copies[r, i].start()
+        ein[x, part, :] = (mm(srx[part, :], qt[x]) + qo[x, part, :]).astype(BF16)
 
     mean_ones = jnp.full((128, 128), 1.0 / 128.0, BF16)
     n_copies = []
     for r in (0, 1, 3, 2):
         head = lax.rem(x + NX - r, NX)
         if r > 0:
-            e_copies[r].wait_recv()
+            for i in range(RCH):
+                e_copies[r, i].wait_recv()
         att = mmt(qfin[head], ein[head]) + lfin[head]
         ms = mm((att * att).astype(BF16), mean_ones)
         nrm = (att * lax.rsqrt(ms + 1e-05) * sg[head]).astype(BF16)
@@ -510,15 +571,16 @@
         v((NP, 256, 128), BF16), v((NP, 256, 128), BF16),
         v((HEADS, 256, 128), BF16), v((HEADS, 128, 128), BF16), v((HEADS, 128, 128), F32),
         v((HEADS, 256, 128), BF16), v((NX, 256, 128), BF16),
+        v((HEADS, 32, 128), F32), v((NX, 32, 128), F32), v((NX, 8, 128), F32), v((NX, 256, 128), BF16),
         v((NX, 128, 128), BF16), v((NX, 128, 128), F32), v((NX, 128, 128), BF16), v((NX, 128, 128), F32),
         v((128, 128), BF16), v((128, 128), F32), v((256, 128), BF16), v((256, 128), BF16),
         v((128, 128), BF16), v((128, 128), BF16), v((NX - 1, 128, 128), BF16), v((NX, 128, 128), BF16),
         v((HEADS, 256, 128), BF16), v((HEADS, 256, 128), F32), v((HEADS, 256, 128), F32),
         v((2, 128, 512), BF16), v((128, 512), BF16), v((128, 4096), F32),
         v((NBLK, NY, 32, BLK), BF16), v((NBLK, 32, BLK), BF16), v((NBLK, 32, BLK), BF16),
-        dma((8,)), dma((2,)), dma((2,)), dma((3,)), dma((3,)), dma((RCH, nz - LOW)), dma((RCH,)),
+        dma((8,)), dma((2,)), dma((2,)), dma((3,)), dma((3,)), dma((3,)), dma((3,)), dma((RCH, nz - LOW)), dma((RCH,)),
         dma((PCH,)), dma((PCH,)), pltpu.SemaphoreType.REGULAR, dma((NBLK,)),
-        dma((3,)), dma((3,)), dma((4,)), dma((4,)), dma((3, NBLK)), dma((3, NBLK)),
+        dma((3, RCH)), dma((3, RCH)), dma((4,)), dma((4,)), dma((3, NBLK)), dma((3, NBLK)),
     ]
     half = jax.ShapeDtypeStruct((32, 4096), BF16)
     own, one, two = pl.pallas_call(

time: 47.4 us -> 47.9 us (1.011); the launches traced: 47.3 us -> 47.1 us
  no operation moved by 1% of the time
where the time goes in v4:
time: 47.9 us; the launch traced here: 47.1 us
  Pallas kernels  45.2 us (94%)
  other arithmetic  1.91 us (4%)
    pallas_call x1, Pallas kernels, body(): pl.pallas_call(functools.partial(kernel, nz), out_shape=(half, half, half...  45.2 us
    convert_element_type x1, other arithmetic, body(): return (own.astype(F32) + one.astype(F32) + two.astype(F32)).astype(BF16)  1.91 us

profile of v4, /device:TPU:226, one launch (start us, length us, event | category | flops | bytes accessed | tf_op | source)
XLA Modules:
  0.0 47.1 jit_solution(1499675627563989692)
XLA Ops:
  0.0 45.2 %shard_map.82 = (bf16[32,4096]{1,0:T(8,128)(2,1)}, bf16[32,4096]{1,0:T(8,128)(2,1)}, bf16[32,4096]{1,0:T(8,128)(2,1)}) custom-call(bf16[3,256,512]{2,1,0:T(8,128)(2,1)} %proj_hbm.1, f32[3,4,512]{2,1,0:T(4,128)} %cw_hbm.1, f32[4,256]{1,0:T(4,128)} %ld_hbm.1, f32[4,256]{1,0:T(4,128)} %wr_hbm.1, s32[2,8]{1,0:T(2,128)} %bitcast.2, bf16[256,512]{1,0:T(8,128)(2,1)} %gate_hbm.1, ...), custom_call_target="tpu_custom_call" | custom-call | tf_op jit(solution)/shard_map/pallas_call | solution.py:586
  45.2 1.9 %add_convert_fusion = bf16[32,4096]{1,0:T(8,128)(2,1)} fusion(bf16[32,4096]{1,0:T(8,128)(2,1)} %get-tuple-element.10, bf16[32,4096]{1,0:T(8,128)(2,1)} %get-tuple-element.9, bf16[32,4096]{1,0:T(8,128)(2,1)} %get-tuple-element.8), kind=kLoop, calls=%fused_computation | loop fusion | flops 786432 | bytes 1048576 | tf_op jit(solution)/shard_map/convert_element_type | solution.py:599

commit v5 on v4

--- a/solution.py
+++ b/solution.py
@@ -16,12 +16,10 @@
 NY = 4
 HEADS = 4
 NP = 8
-BLK = 512
-NBLK = 8
-RCH = 4
-PCH = 4
+BLK = 1024
+NBLK = 4
+RCH = 1
 HEAD = 4
-LOW = 3
 
 
 def mm(a, b):
@@ -41,7 +39,7 @@
     cw_ref, ld_ref, wr_ref, db_ref, gain_ref,
     proj, halo, ext, gate, w_own, w_par,
     gbuf, cbuf, masks, kq, rt, vb, lb, pb_s, xb, yb, xc, wub, wts, t1o1, t2, o2, tos, tin, am, ain, ab, mb,
-    pt, po, qt, qo, rowt, rowo, prx, psnd, srx, snd, es, ein, qfin, lfin, sg,
+    pt, po, qt, qo, rowm, abuf, bbuf, mid, prx, srx, snd, es, ein, qfin, lfin, sg,
     nb, nrx, acc, pb, rxo, cs,
     lsem, hsem, wsem, xs_sem, xr_sem, as_sem, ar_sem, zs_sem, zr_sem, ps_sem, pr_sem, rdy, fsem, es_sem, er_sem, ns_sem, nr_sem, rs_sem, rr_sem,
 ):
@@ -203,13 +201,16 @@
         loads[2].start()
         w_copy.start()
 
-        @pl.when(z == LOW + 1)
+        @pl.when((z == 1) | (z == 6))
         def _():
             pl.semaphore_signal(rdy, inc=1, device_id=(zdn * NX + x, tp), device_id_type=MESH)
 
-        @pl.when(z == nz - 1)
+    def word_from_above(row):
+        @pl.when(z == row)
         def _():
-            pl.semaphore_signal(rdy, inc=1, device_id=(zup * NX + x, tp), device_id_type=MESH)
+            pl.semaphore_wait(rdy, 1)
+            if row > 2:
+                pl.semaphore_signal(rdy, inc=1, device_id=(zdn * NX + x, tp), device_id_type=MESH)
 
     loads[0].wait()
     for span in (1, 0):
@@ -259,10 +260,7 @@
         x_copies.append(copy)
     tin[x] = tos[x]
 
-    @pl.when(z == LOW)
-    def _():
-        pl.semaphore_wait(rdy, 1)
-        pl.semaphore_signal(rdy, inc=1, device_id=(zdn * NX + x, tp), device_id_type=MESH)
+    word_from_above(5)
 
     halo_copy.wait()
     for s in (1, 2):
@@ -300,6 +298,7 @@
         copy.start()
         a_copies.append(copy)
     ain[x] = am[x]
+    word_from_above(4)
 
     corner = (row_i < HEAD) & (col_i < HEAD)
     below = (row_i >= HEAD) & (col_i < HEAD)
@@ -323,6 +322,8 @@
         updates(p)
     for p in first_span:
         maps(p)
+
+    word_from_above(3)
 
     for span in range(2):
         before = halo[0, 8:16, :] if span == 0 else proj[0, SPAN - 8 : SPAN, :]
@@ -345,6 +346,8 @@
                 q2 = mmt(q.astype(BF16), t1o1[h])
                 qfin[h, 128:256, :] = q2[:, 0:128].astype(BF16)
                 lfin[h, 128:256, :] = pw[:, 128:256] + q2[:, 128:256]
+    word_from_above(2)
+    word_from_above(0)
     loads[1].wait()
     for h in range(HEADS):
         cols = pl.ds(h * 128, 128)
@@ -370,109 +373,122 @@
     for j in range(1, NX):
         step = mm(cur, mb[j, 0:128, :])
         off = step[128:256] + mb[j, 128:256, :].astype(F32)
-        if j < NX - 1:
-            pt[j + 1] = step[0:128].astype(BF16)
-            po[j + 1] = off
-            cur = jnp.concatenate([step[0:128], off], axis=0).astype(BF16)
-        else:
-            rowt[...] = step[0:128].astype(BF16)
-            rowo[...] = off
+        pt[j + 1] = step[0:128].astype(BF16)
+        po[j + 1] = off
+        cur = jnp.concatenate([step[0:128], off], axis=0).astype(BF16)
+    rowm[...] = cur
 
     crows = 128 // RCH
-    prows = 256 // PCH
 
     def s_copy(i, to, k):
         part = pl.ds(i * crows, crows)
         return remote(snd.at[part, :], srx.at[part, :], zs_sem.at[i, k], zr_sem.at[i], (to * NX + x, tp))
 
-    def p_copy(i):
-        part = pl.ds(i * prows, prows)
-        return remote(psnd.at[part, :], prx.at[part, :], ps_sem.at[i], pr_sem.at[i], (zup * NX + x, tp))
+    def m_copy(src, dst, k, slot, to):
+        return remote(src, dst, ps_sem.at[k], pr_sem.at[slot], (to * NX + x, tp))
+
+    def chain(first, second):
+        new = mm(first[...], second[0:128, :])
+        return new[0:128], new[128:256] + second[128:256, :].astype(F32)
 
     @pl.when(z == 0)
     def _():
-        snd[...] = rowo[...].astype(BF16)
-        pl.semaphore_wait(rdy, 1)
+        snd[...] = po[NX].astype(BF16)
         for i in range(RCH):
-            s_copy(i, zup, 0).start()
+            s_copy(i, 2, 1).start()
+            s_copy(i, 1, 0).start()
         srx[...] = jnp.zeros((128, 128), BF16)
 
-    @pl.when(z == LOW)
-    def _():
-        psnd[0:128, :] = rowt[...]
-        psnd[128:256, :] = rowo[...].astype(BF16)
-        for i in range(PCH):
-            p_copy(i).start()
-
-    @pl.when(z <= LOW)
-    def _():
-        prx[0:128, :] = eye_f.astype(BF16)
-        prx[128:256, :] = jnp.zeros((128, 128), BF16)
-
-    @pl.when(z > LOW)
-    def _():
-        for i in range(PCH):
-            part = pl.ds(i * prows, prows)
-            p_copy(i).wait_recv()
-
-            @pl.when(z < nz - 1)
-            def _():
-                new = mm(prx[part, :], rowt[...])
-                if i * prows >= 128:
-                    new = new + rowo[i * prows - 128 : (i + 1) * prows - 128, :]
-                psnd[part, :] = new.astype(BF16)
-                p_copy(i).start()
-
-    for j in range(NX):
+    @pl.when(z == 1)
+    def _():
+        m_copy(rowm, abuf, 0, 0, 2).start()
+
+    @pl.when(z == 3)
+    def _():
+        m_copy(rowm, abuf, 0, 0, 4).start()
+        m_copy(rowm, abuf, 1, 0, 5).start()
+
+    @pl.when(z == 4)
+    def _():
+        m_copy(rowm, bbuf, 0, 1, 5).start()
+
+    @pl.when(z == 5)
+    def _():
+        m_copy(rowm, bbuf, 0, 1, 6).start()
+
+    @pl.when((z == 0) | (z == 1) | (z == 3))
+    def _():
+        abuf[0:128, :] = eye_f.astype(BF16)
+        abuf[128:256, :] = jnp.zeros((128, 128), BF16)
+
+    @pl.when(z < 5)
+    def _():
+        bbuf[0:128, :] = eye_f.astype(BF16)
+        bbuf[128:256, :] = jnp.zeros((128, 128), BF16)
+
+    @pl.when(z == 4)
+    def _():
+        m_copy(rowm, abuf, 0, 0, 4).wait_recv()
+        t, o = chain(abuf, rowm)
+        mid[0:128, :] = t.astype(BF16)
+        mid[128:256, :] = o.astype(BF16)
+        m_copy(mid, abuf, 1, 0, 7).start()
+        m_copy(mid, abuf, 2, 0, 6).start()
+
+    @pl.when(z == 6)
+    def _():
+        m_copy(rowm, bbuf, 0, 1, 6).wait_recv()
+        t, o = chain(bbuf, rowm)
+        mid[0:128, :] = t.astype(BF16)
+        mid[128:256, :] = o.astype(BF16)
+        m_copy(mid, bbuf, 0, 1, 7).start()
+
+    @pl.when((z == 2) | (z > 4))
+    def _():
+        m_copy(rowm, abuf, 0, 0, 2).wait_recv()
+
+    @pl.when((z == 5) | (z == 7))
+    def _():
+        m_copy(rowm, bbuf, 0, 1, 5).wait_recv()
+
+    t, o = chain(abuf, bbuf)
+    prx[0:128, :] = t.astype(BF16)
+    prx[128:256, :] = o.astype(BF16)
+    for j in range(NX + 1):
         new = mm(prx[...], pt[j])
         qt[j] = new[0:128].astype(BF16)
         qo[j] = new[128:256] + po[j]
 
-    @pl.when(z == LOW - 1)
-    def _():
-        pl.semaphore_wait(rdy, 1)
-
-    def e_copy(r, i, to_x):
-        part = pl.ds(i * crows, crows)
-        return remote(
-            es.at[r - 1, part, :], ein.at[x, part, :], es_sem.at[r - 1, i], er_sem.at[r - 1, i], (z * NX + to_x, tp)
-        )
-
-    e_copies = {}
     for i in range(RCH):
         part = pl.ds(i * crows, crows)
 
         @pl.when(z > 0)
         def _():
-            s_copy(i, zup, 0).wait_recv()
-
-        @pl.when((z > 0) & (z < LOW))
+            s_copy(i, 1, 0).wait_recv()
+
+        @pl.when(z == 2)
         def _():
-            snd[part, :] = (mm(srx[part, :], rowt[...]) + rowo[part, :]).astype(BF16)
-
-        @pl.when((z > 0) & (z < LOW - 1))
-        def _():
-            s_copy(i, zup, 0).start()
-
-        @pl.when(z == LOW - 1)
-        def _():
-            for far in range(nz - 1, LOW - 1, -1):
-                s_copy(i, far, far - LOW).start()
-
-        for r in (2, 1, 3):
-            to_x = lax.rem(x + r, NX)
-            es[r - 1, part, :] = (mm(srx[part, :], qt[to_x]) + qo[to_x, part, :]).astype(BF16)
-            e_copies[r, i] = e_copy(r, i, to_x)
-            e_copies[r, i].start()
-        ein[x, part, :] = (mm(srx[part, :], qt[x]) + qo[x, part, :]).astype(BF16)
+            snd[part, :] = (mm(srx[part, :], qt[NX]) + qo[NX, part, :]).astype(BF16)
+            for far in range(7, 2, -1):
+                s_copy(i, far, far - 3).start()
+
+    def e_copy(r, i, to_x):
+        return remote(es.at[r - 1], ein.at[x], es_sem.at[r - 1, i], er_sem.at[r - 1, i], (z * NX + to_x, tp))
+
+    e_copies = {}
+    for r in (2, 1, 3):
+        to_x = lax.rem(x + r, NX)
+        es[r - 1] = (mm(srx[...], qt[to_x]) + qo[to_x]).astype(BF16)
+        e_copies[r, 0] = e_copy(r, 0, to_x)
+        e_copies[r, 0].start()
+    ein[x] = (mm(srx[...], qt[x]) + qo[x]).astype(BF16)
 
     mean_ones = jnp.full((128, 128), 1.0 / 128.0, BF16)
     n_copies = []
     for r in (0, 1, 3, 2):
         head = lax.rem(x + NX - r, NX)
         if r > 0:
-            for i in range(RCH):
-                e_copies[r, i].wait_recv()
+            e_copies[r, 0].wait_recv()
         att = mmt(qfin[head], ein[head]) + lfin[head]
         ms = mm((att * att).astype(BF16), mean_ones)
         nrm = (att * lax.rsqrt(ms + 1e-05) * sg[head]).astype(BF16)
@@ -495,7 +511,7 @@
     for copy in n_copies:
         copy.wait()
 
-    order = (0, 4, 1, 5, 2, 6, 3, 7)
+    order = (0, 2, 1, 3)
     half = NBLK // 2
     o_copies, d_copies, c_copies, f_copies = {}, {}, {}, []
     for b in order:
@@ -530,21 +546,18 @@
     for copy in f_copies:
         copy.wait()
 
-    @pl.when(z < LOW - 1)
-    def _():
-        for i in range(RCH):
-            s_copy(i, zup, 0).wait_send()
-
-    @pl.when(z == LOW - 1)
-    def _():
-        for i in range(RCH):
-            for far in range(LOW, nz):
-                s_copy(i, far, far - LOW).wait_send()
-
-    @pl.when((z >= LOW) & (z < nz - 1))
-    def _():
-        for i in range(PCH):
-            p_copy(i).wait_send()
+    for row, count in ((0, 2), (2, 5)):
+        @pl.when(z == row)
+        def _():
+            for i in range(RCH):
+                for k in range(count):
+                    s_copy(i, 1, k).wait_send()
+
+    for row, count in ((1, 1), (3, 2), (4, 3), (5, 1), (6, 1)):
+        @pl.when(z == row)
+        def _():
+            for k in range(count):
+                m_copy(rowm, abuf, k, 0, 2).wait_send()
 
     for copy in e_copies.values():
         copy.wait_send()
@@ -572,15 +585,16 @@
         v((HEADS, 256, 128), BF16), v((HEADS, 128, 128), BF16), v((HEADS, 128, 128), F32),
         v((HEADS, 256, 128), BF16), v((NX, 256, 128), BF16),
         v((HEADS, 32, 128), F32), v((NX, 32, 128), F32), v((NX, 8, 128), F32), v((NX, 256, 128), BF16),
-        v((NX, 128, 128), BF16), v((NX, 128, 128), F32), v((NX, 128, 128), BF16), v((NX, 128, 128), F32),
-        v((128, 128), BF16), v((128, 128), F32), v((256, 128), BF16), v((256, 128), BF16),
+        v((NX + 1, 128, 128), BF16), v((NX + 1, 128, 128), F32), v((NX + 1, 128, 128), BF16),
+        v((NX + 1, 128, 128), F32), v((256, 128), BF16), v((256, 128), BF16), v((256, 128), BF16),
+        v((256, 128), BF16), v((256, 128), BF16),
         v((128, 128), BF16), v((128, 128), BF16), v((NX - 1, 128, 128), BF16), v((NX, 128, 128), BF16),
         v((HEADS, 256, 128), BF16), v((HEADS, 256, 128), F32), v((HEADS, 256, 128), F32),
         v((2, 128, 512), BF16), v((128, 512), BF16), v((128, 4096), F32),
         v((NBLK, NY, 32, BLK), BF16), v((NBLK, 32, BLK), BF16), v((NBLK, 32, BLK), BF16),
-        dma((8,)), dma((2,)), dma((2,)), dma((3,)), dma((3,)), dma((3,)), dma((3,)), dma((RCH, nz - LOW)), dma((RCH,)),
-        dma((PCH,)), dma((PCH,)), pltpu.SemaphoreType.REGULAR, dma((NBLK,)),
-        dma((3, RCH)), dma((3, RCH)), dma((4,)), dma((4,)), dma((3, NBLK)), dma((3, NBLK)),
+        dma((8,)), dma((2,)), dma((2,)), dma((3,)), dma((3,)), dma((3,)), dma((3,)), dma((RCH, 5)), dma((RCH,)),
+        dma((3,)), dma((2,)), pltpu.SemaphoreType.REGULAR, dma((NBLK,)),
+        dma((3, 1)), dma((3, 1)), dma((4,)), dma((4,)), dma((3, NBLK)), dma((3, NBLK)),
     ]
     half = jax.ShapeDtypeStruct((32, 4096), BF16)
     own, one, two = pl.pallas_call(
@@ -612,6 +626,7 @@
     )
     out_specs = P(("ctx", "tp"), None)
     nz = mesh.shape["ctx"] // NX
+    assert nz == 8
     return jax.shard_map(
         functools.partial(body, nz), mesh=mesh, in_specs=in_specs, out_specs=out_specs, check_vma=False
     )

time: 47.9 us -> 43.3 us (0.904)
  Pallas kernels: 45.2 us -> 40.7 us
    pallas_call x1, Pallas kernels: 45.2 us -> 40.7 us  [body(): pl.pallas_call(functools.partial(kernel, nz), out_shape=(half, half, half...]
where the time goes in v5:
time: 43.3 us; the launch traced here: 42.6 us
  Pallas kernels  40.7 us (94%)
  other arithmetic  1.91 us (4%)
    pallas_call x1, Pallas kernels, body(): pl.pallas_call(functools.partial(kernel, nz), out_shape=(half, half, half...  40.7 us
    convert_element_type x1, other arithmetic, body(): return (own.astype(F32) + one.astype(F32) + two.astype(F32)).astype(BF16)  1.91 us

profile of v5, /device:TPU:226, one launch (start us, length us, event | category | flops | bytes accessed | tf_op | source)
XLA Modules:
  0.0 42.6 jit_solution(5260837897896376082)
XLA Ops:
  0.0 40.7 %shard_map.82 = (bf16[32,4096]{1,0:T(8,128)(2,1)}, bf16[32,4096]{1,0:T(8,128)(2,1)}, bf16[32,4096]{1,0:T(8,128)(2,1)}) custom-call(bf16[3,256,512]{2,1,0:T(8,128)(2,1)} %proj_hbm.1, f32[3,4,512]{2,1,0:T(4,128)} %cw_hbm.1, f32[4,256]{1,0:T(4,128)} %ld_hbm.1, f32[4,256]{1,0:T(4,128)} %wr_hbm.1, s32[2,8]{1,0:T(2,128)} %bitcast.2, bf16[256,512]{1,0:T(8,128)(2,1)} %gate_hbm.1, ...), custom_call_target="tpu_custom_call" | custom-call | tf_op jit(solution)/shard_map/pallas_call | solution.py:600
  40.7 1.9 %add_convert_fusion = bf16[32,4096]{1,0:T(8,128)(2,1)} fusion(bf16[32,4096]{1,0:T(8,128)(2,1)} %get-tuple-element.10, bf16[32,4096]{1,0:T(8,128)(2,1)} %get-tuple-element.9, bf16[32,4096]{1,0:T(8,128)(2,1)} %get-tuple-element.8), kind=kLoop, calls=%fused_computation | loop fusion | flops 786432 | bytes 1048576 | tf_op jit(solution)/shard_map/convert_element_type | solution.py:613

commit v6 on v5

--- a/solution.py
+++ b/solution.py
@@ -35,13 +35,13 @@
 
 
 def kernel(
-    nz, proj_hbm, cw_hbm, ld_hbm, wr_hbm, db_hbm, gate_hbm, gain_hbm, w_hbm, own_out, rx1, rx2,
+    nz, proj_hbm, cw_hbm, ld_hbm, wr_hbm, db_hbm, gate_hbm, gain_hbm, w_hbm, out_ref,
     cw_ref, ld_ref, wr_ref, db_ref, gain_ref,
     proj, halo, ext, gate, w_own, w_par,
     gbuf, cbuf, masks, kq, rt, vb, lb, pb_s, xb, yb, xc, wub, wts, t1o1, t2, o2, tos, tin, am, ain, ab, mb,
     pt, po, qt, qo, rowm, abuf, bbuf, mid, prx, srx, snd, es, ein, qfin, lfin, sg,
-    nb, nrx, acc, pb, rxo, cs,
-    lsem, hsem, wsem, xs_sem, xr_sem, as_sem, ar_sem, zs_sem, zr_sem, ps_sem, pr_sem, rdy, fsem, es_sem, er_sem, ns_sem, nr_sem, rs_sem, rr_sem,
+    nb, nrx, acc, pb, rxo, rx1, rx2, cs,
+    lsem, hsem, wsem, xs_sem, xr_sem, as_sem, ar_sem, zs_sem, zr_sem, ps_sem, pr_sem, rdy, es_sem, er_sem, ns_sem, nr_sem, rs_sem, rr_sem,
 ):
     ctx = lax.axis_index("ctx")
     tp = lax.axis_index("tp")
@@ -513,7 +513,7 @@
 
     order = (0, 2, 1, 3)
     half = NBLK // 2
-    o_copies, d_copies, c_copies, f_copies = {}, {}, {}, []
+    o_copies, d_copies, c_copies = {}, {}, {}
     for b in order:
         cols = pl.ds(b * BLK, BLK)
         res = (acc[:, cols] + mm(nrx[...], w_par[:, cols])).astype(BF16)
@@ -528,8 +528,6 @@
             pb.at[b, second], rx1.at[:, cols], rs_sem.at[1, b], rr_sem.at[1, b], (ctx, second * 2 + core)
         )
         d_copies[b].start()
-        f_copies.append(pltpu.make_async_copy(pb.at[b, y], own_out.at[:, cols], fsem.at[b]))
-        f_copies[-1].start()
     for b in order:
         first = right if b < half else left
         cols = pl.ds(b * BLK, BLK)
@@ -542,9 +540,9 @@
     for b in order:
         d_copies[b].wait_recv()
         c_copies[b].wait_recv()
-
-    for copy in f_copies:
-        copy.wait()
+        cols = pl.ds(b * BLK, BLK)
+        total = pb[b, y].astype(F32) + rx1[:, cols].astype(F32) + rx2[:, cols].astype(F32)
+        out_ref[:, cols] = total.astype(BF16)
 
     for row, count in ((0, 2), (2, 5)):
         @pl.when(z == row)
@@ -591,17 +589,17 @@
         v((128, 128), BF16), v((128, 128), BF16), v((NX - 1, 128, 128), BF16), v((NX, 128, 128), BF16),
         v((HEADS, 256, 128), BF16), v((HEADS, 256, 128), F32), v((HEADS, 256, 128), F32),
         v((2, 128, 512), BF16), v((128, 512), BF16), v((128, 4096), F32),
-        v((NBLK, NY, 32, BLK), BF16), v((NBLK, 32, BLK), BF16), v((NBLK, 32, BLK), BF16),
+        v((NBLK, NY, 32, BLK), BF16), v((NBLK, 32, BLK), BF16), v((32, 4096), BF16), v((32, 4096), BF16),
+        v((NBLK, 32, BLK), BF16),
         dma((8,)), dma((2,)), dma((2,)), dma((3,)), dma((3,)), dma((3,)), dma((3,)), dma((RCH, 5)), dma((RCH,)),
-        dma((3,)), dma((2,)), pltpu.SemaphoreType.REGULAR, dma((NBLK,)),
+        dma((3,)), dma((2,)), pltpu.SemaphoreType.REGULAR,
         dma((3, 1)), dma((3, 1)), dma((4,)), dma((4,)), dma((3, NBLK)), dma((3, NBLK)),
     ]
-    half = jax.ShapeDtypeStruct((32, 4096), BF16)
-    own, one, two = pl.pallas_call(
+    return pl.pallas_call(
         functools.partial(kernel, nz),
-        out_shape=(half, half, half),
+        out_shape=pltpu.VMEM((32, 4096), BF16),
         in_specs=[aspec] * 8,
-        out_specs=(aspec, aspec, aspec),
+        out_specs=vspec,
         scratch_shapes=scratch,
         compiler_params=pltpu.CompilerParams(
             collective_id=0, has_side_effects=True, vmem_limit_bytes=56 * 1024 * 1024
@@ -610,7 +608,6 @@
         projected, conv_weight, log_decay, write_rate, doc_bounds.T, out_gate,
         norm_gain.reshape(1, -1), out_weight,
     )
-    return (own.astype(F32) + one.astype(F32) + two.astype(F32)).astype(BF16)
 
 
 def solution(mesh):

time: 43.3 us -> 42 us (0.970)
  other arithmetic: 1.91 us -> 0 us
  local copies, waits for them, and re-layouts: 0 us -> 0.71 us
    convert_element_type x1 -> x0, other arithmetic: 1.91 us -> none  [body(): return (own.astype(F32) + one.astype(F32) + two.astype(F32)).astype(BF16)]
    unnamed x0 -> x1, local copies, waits for them, and re-layouts: none -> 0.71 us
where the time goes in v6:
time: 42 us; the launch traced here: 41.3 us
  Pallas kernels  40.6 us (97%)
  local copies, waits for them, and re-layouts  0.71 us (2%)
    pallas_call x1, Pallas kernels, body(): pl.pallas_call(functools.partial(kernel, nz), out_shape=pltpu.VMEM((32, 4...  40.6 us

profile of v6, /device:TPU:226, one launch (start us, length us, event | category | flops | bytes accessed | tf_op | source)
XLA Modules:
  0.0 41.3 jit_solution(10043754345975836282)
XLA Ops:
  0.0 40.6 %shard_map.82 = bf16[32,4096]{1,0:T(8,128)(2,1)S(1)} custom-call(bf16[3,256,512]{2,1,0:T(8,128)(2,1)} %proj_hbm.1, f32[3,4,512]{2,1,0:T(4,128)} %cw_hbm.1, f32[4,256]{1,0:T(4,128)} %ld_hbm.1, f32[4,256]{1,0:T(4,128)} %wr_hbm.1, s32[2,8]{1,0:T(2,128)} %bitcast.2, bf16[256,512]{1,0:T(8,128)(2,1)} %gate_hbm.1, f32[1,128]{1,0:T(1,128)} %bitcast.3, ...), custom_call_target="tpu_custom_call" | custom-call | tf_op jit(solution)/shard_map/pallas_call | solution.py:598
  40.6 0.7 %copy.10 = bf16[32,4096]{1,0:T(8,128)(2,1)} copy(bf16[32,4096]{1,0:T(8,128)(2,1)S(1)} %shard_map.82) | data formatting | bytes 524288

commit v7 on v6

--- a/solution.py
+++ b/solution.py
@@ -38,7 +38,7 @@
     nz, proj_hbm, cw_hbm, ld_hbm, wr_hbm, db_hbm, gate_hbm, gain_hbm, w_hbm, out_ref,
     cw_ref, ld_ref, wr_ref, db_ref, gain_ref,
     proj, halo, ext, gate, w_own, w_par,
-    gbuf, cbuf, masks, kq, rt, vb, lb, pb_s, xb, yb, xc, wub, wts, t1o1, t2, o2, tos, tin, am, ain, ab, mb,
+    gbuf, cbuf, masks, kq, rt, vb, lb, pb_s, xb, yb, xc, wub, wts, t1o1, t2, o2, tos, tin, am, amb, ain, ab, mb,
     pt, po, qt, qo, rowm, abuf, bbuf, mid, prx, srx, snd, es, ein, qfin, lfin, sg,
     nb, nrx, acc, pb, rxo, rx1, rx2, cs,
     lsem, hsem, wsem, xs_sem, xr_sem, as_sem, ar_sem, zs_sem, zr_sem, ps_sem, pr_sem, rdy, es_sem, er_sem, ns_sem, nr_sem, rs_sem, rr_sem,
@@ -191,12 +191,19 @@
     second_span = range(HEADS, NP)
 
     rows = proj_hbm.shape[1]
-    halo_copy = remote(proj_hbm.at[:, pl.ds(rows - 16, 16), :], halo, hsem.at[0], hsem.at[1], (nxt, tp))
+    last_rows = pl.ds(rows - 8, 8)
+    halo_copy = remote(
+        proj_hbm.at[pl.ds(1, 2), last_rows, :], halo.at[pl.ds(1, 2)], hsem.at[0], hsem.at[1], (nxt, tp)
+    )
+    halo_query = remote(
+        proj_hbm.at[pl.ds(0, 1), last_rows, :], halo.at[pl.ds(0, 1)], hsem.at[2], hsem.at[3], (nxt, tp)
+    )
     w_copy = remote(w_hbm, w_par, wsem.at[0], wsem.at[1], (ctx, y * 2 + other))
 
     def enter():
         pl.semaphore_wait(barrier, len(peers))
         halo_copy.start()
+        halo_query.start()
         loads[1].start()
         loads[2].start()
         w_copy.start()
@@ -264,7 +271,7 @@
 
     halo_copy.wait()
     for s in (1, 2):
-        ext[s, 0:8, :] = halo[s, 8:16, :].astype(F32) * keeps[0]
+        ext[s, 0:8, :] = halo[s].astype(F32) * keeps[0]
     fill((1, 2), 0, 0, 16)
     for h in range(HEADS):
         keys = kq[h, 0:16, :].astype(F32)
@@ -290,14 +297,17 @@
             am[h, 8 + i : 9 + i, :] = us[i]
         tail = jnp.exp(end - gcol[0:8]) * keys[0:8]
         am[h, 16:24, :] = jnp.where(row_i[0:8] < HEAD, tail, 0.0)
-        am[h, 24:32, :] = keeps[0] * jnp.exp(end)
+        decay = keeps[0] * jnp.exp(end)
+        high = decay.astype(BF16).astype(F32)
+        am[h, 24:32, :] = jnp.where(row_i[0:8] < 4, high, decay - high)
+        amb[h] = am[h].astype(BF16)
     a_copies = []
     for r in (2, 1, 3):
         to_x = lax.rem(x + r, NX)
-        copy = remote(am.at[to_x], ain.at[x], as_sem.at[r - 1], ar_sem.at[r - 1], (z * NX + to_x, tp))
+        copy = remote(amb.at[to_x], ain.at[x], as_sem.at[r - 1], ar_sem.at[r - 1], (z * NX + to_x, tp))
         copy.start()
         a_copies.append(copy)
-    ain[x] = am[x]
+    ain[x] = amb[x]
     word_from_above(4)
 
     corner = (row_i < HEAD) & (col_i < HEAD)
@@ -325,8 +335,9 @@
 
     word_from_above(3)
 
+    halo_query.wait()
     for span in range(2):
-        before = halo[0, 8:16, :] if span == 0 else proj[0, SPAN - 8 : SPAN, :]
+        before = halo[0] if span == 0 else proj[0, SPAN - 8 : SPAN, :]
         ext[0, 0:8, :] = before.astype(F32) * keeps[span]
         ext[0, 8:136, :] = proj[0, span * SPAN : span * SPAN + SPAN, :].astype(F32)
         fill((0,), span, 0, SPAN)
@@ -358,12 +369,14 @@
     for copy in a_copies:
         copy.wait()
 
+    parts = [ain[j].astype(F32) for j in range(NX)]
     for j in range(NX):
-        ab[j] = mm(ain[j, 16:24, :].astype(BF16), tin[j, 0:128, :])
+        ab[j] = mm(parts[j][16:24].astype(BF16), tin[j, 0:128, :])
     for j in range(NX):
-        wu = jnp.concatenate([ain[j, 0:8, :], ain[j, 8:16, :]], axis=1).astype(BF16)
+        wu = jnp.concatenate([parts[j][0:8], parts[j][8:16]], axis=1).astype(BF16)
         low = lax.dot_general(wu, ab[j].astype(BF16), (((0,), (0,)), ((), ())), preferred_element_type=F32)
-        mb[j, 0:128, :] = (tin[j, 0:128, :].astype(F32) * ain[j, 24:25, :] + low[0:128]).astype(BF16)
+        decay = parts[j][24:25] + parts[j][28:29]
+        mb[j, 0:128, :] = (tin[j, 0:128, :].astype(F32) * decay + low[0:128]).astype(BF16)
         mb[j, 128:256, :] = (tin[j, 128:256, :].astype(F32) + low[128:256]).astype(BF16)
     pt[0] = eye_f.astype(BF16)
     po[0] = jnp.zeros((128, 128), F32)
@@ -573,7 +586,7 @@
     scratch = [
         v((3, TAPS, 512), F32), v((HEADS, 256), F32), v((HEADS, 256), F32),
         pltpu.SMEM((2, 8), jnp.int32), v((1, 128), F32),
-        v((3, 256, 512), BF16), v((3, 16, 512), BF16), v((3, 136, 512), F32), v((256, 512), BF16),
+        v((3, 256, 512), BF16), v((3, 8, 512), BF16), v((3, 136, 512), F32), v((256, 512), BF16),
         v((512, 4096), BF16), v((512, 4096), BF16),
         v((128, 128), F32), v((128, 128), F32), v((6, 128, 128), BF16),
         v((NP, 256, 128), BF16), v((NP, 256, 128), BF16), v((NP, 128, 128), BF16),
@@ -582,7 +595,7 @@
         v((NP, 256, 128), BF16), v((NP, 256, 128), BF16),
         v((HEADS, 256, 128), BF16), v((HEADS, 128, 128), BF16), v((HEADS, 128, 128), F32),
         v((HEADS, 256, 128), BF16), v((NX, 256, 128), BF16),
-        v((HEADS, 32, 128), F32), v((NX, 32, 128), F32), v((NX, 8, 128), F32), v((NX, 256, 128), BF16),
+        v((HEADS, 32, 128), F32), v((HEADS, 32, 128), BF16), v((NX, 32, 128), BF16), v((NX, 8, 128), F32), v((NX, 256, 128), BF16),
         v((NX + 1, 128, 128), BF16), v((NX + 1, 128, 128), F32), v((NX + 1, 128, 128), BF16),
         v((NX + 1, 128, 128), F32), v((256, 128), BF16), v((256, 128), BF16), v((256, 128), BF16),
         v((256, 128), BF16), v((256, 128), BF16),
@@ -591,7 +604,7 @@
         v((2, 128, 512), BF16), v((128, 512), BF16), v((128, 4096), F32),
         v((NBLK, NY, 32, BLK), BF16), v((NBLK, 32, BLK), BF16), v((32, 4096), BF16), v((32, 4096), BF16),
         v((NBLK, 32, BLK), BF16),
-        dma((8,)), dma((2,)), dma((2,)), dma((3,)), dma((3,)), dma((3,)), dma((3,)), dma((RCH, 5)), dma((RCH,)),
+        dma((8,)), dma((4,)), dma((2,)), dma((3,)), dma((3,)), dma((3,)), dma((3,)), dma((RCH, 5)), dma((RCH,)),
         dma((3,)), dma((2,)), pltpu.SemaphoreType.REGULAR,
         dma((3, 1)), dma((3, 1)), dma((4,)), dma((4,)), dma((3, NBLK)), dma((3, NBLK)),
     ]

time: 42 us -> 41.8 us (level)
  no operation moved by 1% of the time
where the time goes in v7:
time: 41.8 us; the launch traced here: 41.1 us
  Pallas kernels  40.4 us (97%)
  local copies, waits for them, and re-layouts  0.71 us (2%)
    pallas_call x1, Pallas kernels, body(): pl.pallas_call(functools.partial(kernel, nz), out_shape=pltpu.VMEM((32, 4...  40.4 us

profile of v7, /device:TPU:226, one launch (start us, length us, event | category | flops | bytes accessed | tf_op | source)
XLA Modules:
  0.0 41.1 jit_solution(9081760352026760544)
XLA Ops:
  0.0 40.4 %shard_map.82 = bf16[32,4096]{1,0:T(8,128)(2,1)S(1)} custom-call(bf16[3,256,512]{2,1,0:T(8,128)(2,1)} %proj_hbm.1, f32[3,4,512]{2,1,0:T(4,128)} %cw_hbm.1, f32[4,256]{1,0:T(4,128)} %ld_hbm.1, f32[4,256]{1,0:T(4,128)} %wr_hbm.1, s32[2,8]{1,0:T(2,128)} %bitcast.2, bf16[256,512]{1,0:T(8,128)(2,1)} %gate_hbm.1, f32[1,128]{1,0:T(1,128)} %bitcast.3, ...), custom_call_target="tpu_custom_call" | custom-call | tf_op jit(solution)/shard_map/pallas_call | solution.py:611
  40.4 0.7 %copy.10 = bf16[32,4096]{1,0:T(8,128)(2,1)} copy(bf16[32,4096]{1,0:T(8,128)(2,1)S(1)} %shard_map.82) | data formatting | bytes 524288

commit v8 on v7

--- a/solution.py
+++ b/solution.py
@@ -460,6 +460,15 @@
     def _():
         m_copy(rowm, abuf, 0, 0, 2).wait_recv()
 
+    @pl.when(z == 2)
+    def _():
+        new = mm(abuf[...], pt[NX])
+        end_t, end_o = new[0:128].astype(BF16), new[128:256] + po[NX]
+        s_copy(0, 1, 0).wait_recv()
+        snd[...] = (mm(srx[...], end_t) + end_o).astype(BF16)
+        for far in (6, 7, 5, 4, 3):
+            s_copy(0, far, far - 3).start()
+
     @pl.when((z == 5) | (z == 7))
     def _():
         m_copy(rowm, bbuf, 0, 1, 5).wait_recv()
@@ -467,23 +476,14 @@
     t, o = chain(abuf, bbuf)
     prx[0:128, :] = t.astype(BF16)
     prx[128:256, :] = o.astype(BF16)
-    for j in range(NX + 1):
+    for j in range(NX):
         new = mm(prx[...], pt[j])
         qt[j] = new[0:128].astype(BF16)
         qo[j] = new[128:256] + po[j]
 
-    for i in range(RCH):
-        part = pl.ds(i * crows, crows)
-
-        @pl.when(z > 0)
-        def _():
-            s_copy(i, 1, 0).wait_recv()
-
-        @pl.when(z == 2)
-        def _():
-            snd[part, :] = (mm(srx[part, :], qt[NX]) + qo[NX, part, :]).astype(BF16)
-            for far in range(7, 2, -1):
-                s_copy(i, far, far - 3).start()
+    @pl.when((z > 0) & (z != 2))
+    def _():
+        s_copy(0, 1, 0).wait_recv()
 
     def e_copy(r, i, to_x):
         return remote(es.at[r - 1], ein.at[x], es_sem.at[r - 1, i], er_sem.at[r - 1, i], (z * NX + to_x, tp))

time: 41.8 us -> 41.8 us (level)
  no operation moved by 1% of the time
where the time goes in v8:
time: 41.8 us; the launch traced here: 41.1 us
  Pallas kernels  40.3 us (96%)
  local copies, waits for them, and re-layouts  0.71 us (2%)
    pallas_call x1, Pallas kernels, body(): pl.pallas_call(functools.partial(kernel, nz), out_shape=pltpu.VMEM((32, 4...  40.3 us

profile of v8, /device:TPU:226, one launch (start us, length us, event | category | flops | bytes accessed | tf_op | source)
XLA Modules:
  0.0 41.1 jit_solution(5274294938811742511)
XLA Ops:
  0.0 40.3 %shard_map.82 = bf16[32,4096]{1,0:T(8,128)(2,1)S(1)} custom-call(bf16[3,256,512]{2,1,0:T(8,128)(2,1)} %proj_hbm.1, f32[3,4,512]{2,1,0:T(4,128)} %cw_hbm.1, f32[4,256]{1,0:T(4,128)} %ld_hbm.1, f32[4,256]{1,0:T(4,128)} %wr_hbm.1, s32[2,8]{1,0:T(2,128)} %bitcast.2, bf16[256,512]{1,0:T(8,128)(2,1)} %gate_hbm.1, f32[1,128]{1,0:T(1,128)} %bitcast.3, ...), custom_call_target="tpu_custom_call" | custom-call | tf_op jit(solution)/shard_map/pallas_call | solution.py:611
  40.4 0.7 %copy.10 = bf16[32,4096]{1,0:T(8,128)(2,1)} copy(bf16[32,4096]{1,0:T(8,128)(2,1)S(1)} %shard_map.82) | data formatting | bytes 524288
